TPU v7x, 128 devices: a whole 4x4x4 slice. The times are simulated.
128 devices in a mesh: gy: 32 (over y, x_hi, z), gz: 4 (over x_lo, core).
Axes of the slice: x: 4 (x_hi: 2, x_lo: 2; x = x_hi * 2 + x_lo), y: 4, z: 4, core: 2. Of those that a mesh axis runs over, the one named last changes fastest.
Arguments:
- source: float32 [2, 256, 256, 256], P(None, 'gy', 'gz'), may hold values from -6 to 6
- contrast: float32 [256, 256, 256], P('gy', 'gz'), may hold values from 0.5 to 3
- green: float32 [2, 512, 512, 512], P(None, 'gy', 'gz'), may hold values from -6 to 6
- forward_field: float32 [2, 256, 256, 256], P(None, 'gy', 'gz'), may hold values from -6 to 6
- density: float32 [256, 256], P('gy'), may hold values from 0 to 1
- thresh_index: int32 [64, 16], P('gy'), may hold values from 0 to 2
Outputs:
- adjoint: float32 [2, 256, 256, 256], P(None, 'gy', 'gz')
- projected: float32 [256, 256], P('gy')
- gradient: float32 [256, 256], P('gy')
Inputs may be any that keep to these rules, and one draw needn't show every extreme that they name: `thresh_index`: index of a tile's threshold level.
All inputs are finite; a program needn't handle non-finite values.
Results may differ from a plain program's by a relative error of at most 0.000078.
Values sent between devices are 32-bit elements; how exact they have to be, the bound alone decides.
A program may use at most 192 MiB of HBM per device.

v0:
```python
import math

import jax
import jax.numpy as jnp
from jax import lax
from jax.sharding import PartitionSpec as P

NX = 256
NY = 256
NZ = 256
SLAB = 32
RADIUS = 4
TILE_Y = 4
TILE_X = 16
Z0 = 112


sharpness = 8.0
eps_gap = 11.0


def extended(block, sides, width):
    for axis, dim in sides:
        count = lax.axis_size(axis)
        forward = [(i, i + 1) for i in range(count - 1)]
        backward = [(target, source) for source, target in forward]
        low = lax.ppermute(
            lax.slice_in_dim(block, block.shape[dim] - width, None, axis=dim), axis, forward
        )
        high = lax.ppermute(lax.slice_in_dim(block, 0, width, axis=dim), axis, backward)
        block = jnp.concatenate([low, block, high], axis=dim)
    return block


def filter_matrix(count):
    cells = jnp.arange(count)
    offset = jnp.abs(cells[:, None] - cells[None, :])
    tent_weight = jnp.maximum(RADIUS + 1 - offset, 0).astype(jnp.float32)
    return tent_weight / jnp.sum(tent_weight, axis=1, keepdims=True)


def twiddle(first_index, second_index, extent, sign, factor):
    product_index = first_index[:, None] * second_index[None, :] % extent
    angle = product_index.astype(jnp.float32) * (2.0 * math.pi / extent)
    return (jnp.cos(angle) * factor, jnp.sin(angle) * (sign * factor))


def slot_positions(count, parts, physical):
    slots = count // parts
    number = jnp.arange(count)
    owner = number // slots
    within = number % slots
    return within // physical * (physical * parts) + owner * physical + within % physical


def complex_apply(pair, cosine, sine, form):
    highest = lax.Precision.HIGHEST
    real_part = jnp.einsum(form, pair[0], cosine, precision=highest) - jnp.einsum(
        form, pair[1], sine, precision=highest
    )
    imag_part = jnp.einsum(form, pair[0], sine, precision=highest) + jnp.einsum(
        form, pair[1], cosine, precision=highest
    )
    return jnp.stack([real_part, imag_part])


def complex_product(pair, kernel):
    real_part = pair[0] * kernel[0] - pair[1] * kernel[1]
    imag_part = pair[0] * kernel[1] + pair[1] * kernel[0]
    return jnp.stack([real_part, imag_part])


def shards(source, contrast, green, forward_field, density, thresh_index):
    highest = lax.Precision.HIGHEST
    parts_across = lax.axis_size("gy")
    parts_depth = lax.axis_size("gz")
    local_rows = source.shape[1]
    local_depth = source.shape[2]
    xextent = 2 * NX
    yextent = 2 * NY
    zextent = 2 * NZ
    slots_rows = 2 * local_rows
    slots_depth = 2 * local_depth
    stim_field = source * contrast[None]
    cosine_x, sine_x = twiddle(jnp.arange(NX), jnp.arange(xextent), xextent, -1.0, 1.0)
    spectral = complex_apply(stim_field, cosine_x, sine_x, "yzp,pq->yzq")
    spectral = jnp.pad(spectral, ((0, 0), (0, local_rows), (0, 0), (0, 0)))
    rows_slots = slot_positions(slots_rows * parts_across, parts_across, local_rows)
    cosine_y, sine_y = twiddle(rows_slots, jnp.arange(yextent), yextent, -1.0, 1.0)
    spectral = complex_apply(
        lax.all_to_all(spectral, "gy", split_axis=3, concat_axis=1, tiled=True),
        cosine_y,
        sine_y,
        "yzx,yq->xzq",
    )
    spectral = jnp.pad(spectral, ((0, 0), (0, 0), (0, local_depth), (0, 0)))
    depth_slots = slot_positions(slots_depth * parts_depth, parts_depth, local_depth)
    cosine_z, sine_z = twiddle(depth_slots, jnp.arange(zextent), zextent, -1.0, 1.0)
    spectral = complex_apply(
        lax.all_to_all(spectral, "gz", split_axis=3, concat_axis=2, tiled=True),
        cosine_z,
        sine_z,
        "xzy,zq->xyq",
    )
    spectral = complex_product(spectral, green)
    back_cos_z, back_sin_z = twiddle(jnp.arange(zextent), depth_slots, zextent, 1.0, 1.0 / zextent)
    spatial = complex_apply(spectral, back_cos_z, back_sin_z, "xyq,qz->xyz")
    back_cos_y, back_sin_y = twiddle(jnp.arange(yextent), rows_slots, yextent, 1.0, 1.0 / yextent)
    portion = lax.all_to_all(spatial, "gz", split_axis=3, concat_axis=2, tiled=True)
    portion = portion[:, :, :, :local_depth]
    spatial = complex_apply(portion, back_cos_y, back_sin_y, "xqz,qy->yzx")
    back_cos_x, back_sin_x = twiddle(
        jnp.arange(xextent), jnp.arange(NX), xextent, 1.0, 1.0 / xextent
    )
    portion = lax.all_to_all(spatial, "gy", split_axis=1, concat_axis=3, tiled=True)
    portion = portion[:, :local_rows]
    spatial = complex_apply(portion, back_cos_x, back_sin_x, "yzq,qx->yzx")
    adjoint = source - spatial
    depth_index = lax.axis_index("gz") * local_depth + jnp.arange(local_depth)
    inside = ((depth_index >= Z0) & (depth_index < Z0 + SLAB)).astype(jnp.float32)
    product_field = adjoint[0] * forward_field[0] - adjoint[1] * forward_field[1]
    partial_sum = jnp.einsum("yzx,z->yx", product_field, inside, precision=highest) * (
        eps_gap / SLAB
    )
    sensitivity = lax.psum(partial_sum, "gz")
    row_cells = lax.axis_index("gy") * local_rows + jnp.arange(local_rows)
    row_weight = jnp.zeros((local_rows,), jnp.float32)
    for offset in range(-RADIUS, RADIUS + 1):
        valid = ((row_cells + offset >= 0) & (row_cells + offset < NY)).astype(jnp.float32)
        row_weight = row_weight + float(RADIUS + 1 - abs(offset)) * valid
    filt_x = filter_matrix(NX)
    density_wide = extended(density, (("gy", 0),), RADIUS)
    smooth_rows = jnp.zeros((local_rows, NX), jnp.float32)
    for offset in range(-RADIUS, RADIUS + 1):
        smooth_rows = (
            smooth_rows
            + float(RADIUS + 1 - abs(offset))
            * density_wide[RADIUS + offset : RADIUS + offset + local_rows]
        )
    smooth_rows = smooth_rows / row_weight[:, None]
    filtered = jnp.dot(smooth_rows, filt_x.T, precision=highest)
    levels = 0.35 + 0.1 * thresh_index.astype(jnp.float32)
    threshold = jnp.broadcast_to(
        levels[:, None, :, None], (levels.shape[0], TILE_Y, levels.shape[1], TILE_X)
    ).reshape(local_rows, NX)
    steepness = jnp.tanh(sharpness * (filtered - threshold))
    offset_term = jnp.tanh(sharpness * threshold)
    denominator = offset_term + jnp.tanh(sharpness * (1.0 - threshold))
    projected = (offset_term + steepness) / denominator
    weighted = sharpness * (1.0 - steepness * steepness) / denominator * sensitivity
    across_cols = jnp.dot(weighted, filt_x, precision=highest)
    scaled_rows = across_cols / row_weight[:, None]
    scaled_wide = extended(scaled_rows, (("gy", 0),), RADIUS)
    gradient = jnp.zeros((local_rows, NX), jnp.float32)
    for offset in range(-RADIUS, RADIUS + 1):
        gradient = (
            gradient
            + float(RADIUS + 1 - abs(offset))
            * scaled_wide[RADIUS + offset : RADIUS + offset + local_rows]
        )
    return (adjoint, projected, gradient)


def solution(mesh):
    return jax.shard_map(
        shards,
        mesh=mesh,
        in_specs=(
            P(None, "gy", "gz", None),
            P("gy", "gz", None),
            P(None, "gy", "gz", None),
            P(None, "gy", "gz", None),
            P("gy", None),
            P("gy", None),
        ),
        out_specs=(P(None, "gy", "gz", None), P("gy", None), P("gy", None)),
        check_vma=False,
    )
```

profile of v0, /device:TPU:1, one launch (start us, length us, event | category | flops | bytes accessed | tf_op | source)
XLA Modules:
  0.0 765.6 jit_solution(14632210900737043268)
XLA Ops:
  2.1 3.3 fusion.78
  5.5 3.4 fusion.74
  8.8 3.4 fusion.7
  12.3 3.4 fusion.6
  15.9 3.8 copy.67
  19.7 6.6 pad_bitcast_fusion
  26.3 9.8 %reshape.298 = f32[32,1,32768]{2,1,0:T(1,128)} reshape(f32[512,2,16,64]{3,2,1,0:T(8,128)} %pad_bitcast_fusion) | data formatting | bytes 8388608
  36.1 11.7 %all-to-all-start = ((f32[32,1,32768]{2,1,0:T(1,128)}), f32[32,1,32768]{2,1,0:T(1,128)}, u32[]{:S(2)}, u32[]{:S(2)}) async-start(f32[32,1,32768]{2,1,0:T(1,128)} %reshape.298), calls=%async_computation | async-start | bytes 8388608 | tf_op jit(solution)/shard_map/all_to_all | solution.py:91
  47.8 52.5 %all-to-all-done = f32[32,1,32768]{2,1,0:T(1,128)} async-done(((f32[32,1,32768]{2,1,0:T(1,128)}), f32[32,1,32768]{2,1,0:T(1,128)}, u32[]{:S(2)}, u32[]{:S(2)}) %all-to-all-start) | async-done | bytes 4194336 | tf_op jit(solution)/shard_map/all_to_all | solution.py:91
  100.8 13.7 %reduce = f32[32,32768]{1,0:T(8,128)} reduce(f32[32,1,32768]{2,1,0:T(1,128)} %all-to-all-done, f32[]{:T(128)} %broadcast.993), dimensions={1}, to_apply=%all_to_all.48.reduce_sub_computation | reduce | bytes 8388612 | tf_op jit(solution)/shard_map/all_to_all | solution.py:91
  114.5 7.4 reshape.299
  121.9 8.2 %copy.47 = f32[2,16,64,512]{2,3,1,0:T(8,128)S(1)} copy(f32[2,16,64,512]{2,1,0,3:T(8,128)} %bitcast.197) | data formatting | bytes 8388608 | tf_op jit(solution)/shard_map/all_to_all | solution.py:91
  130.1 2.6 fusion.363
  132.7 2.5 copy.48
  135.2 3.3 copy.49
  138.5 8.8 %fusion.42 = f32[512,64,16]{0,1,2:T(8,128)} fusion(f32[512,64,16]{0,1,2:T(8,128)S(1)} %copy.49, s32[512]{0:T(512)S(1)} %fusion.204), kind=kOutput, calls=%fused_computation.79 | convolution fusion | flops 3224895488 | bytes 4196352 | tf_op jit(solution)/shard_map/yzx,yq->xzq/dot_general | solution.py:58
  147.3 9.0 %fusion.38 = f32[512,64,16]{0,1,2:T(8,128)} fusion(f32[512,64,16]{0,1,2:T(8,128)S(1)} %copy.49, s32[512]{0:T(512)S(1)} %fusion.204), kind=kOutput, calls=%fused_computation.75 | convolution fusion | flops 3225157632 | bytes 4196352 | tf_op jit(solution)/shard_map/yzx,yq->xzq/dot_general | solution.py:61
  156.3 2.5 copy.50
  158.8 2.8 copy.51
  161.7 9.2 %subtract_bitcast_fusion.2 = f32[1,16,64,512]{3,2,1,0:T(8,128)S(1)} fusion(f32[512,64,16]{0,1,2:T(8,128)} %fusion.42, f32[512,64,16]{0,1,2:T(8,128)S(1)} %copy.51, s32[512]{0:T(512)S(1)} %fusion.204), kind=kOutput, calls=%fused_computation.21 | convolution fusion | flops 3225681920 | bytes 6293504 | tf_op jit(solution)/shard_map/yzx,yq->xzq/dot_general | solution.py:58
  170.9 7.9 %add_bitcast_fusion.2 = f32[1,16,64,512]{3,2,1,0:T(8,128)S(1)} fusion(f32[512,64,16]{0,1,2:T(8,128)S(1)} %copy-done.4, f32[512,64,16]{0,1,2:T(8,128)S(1)} %copy.51, s32[512]{0:T(512)S(1)} %fusion.204), kind=kOutput, calls=%fused_computation.20 | convolution fusion | flops 3225419776 | bytes 6293504 | tf_op jit(solution)/shard_map/yzx,yq->xzq/dot_general | solution.py:61
  178.8 2.5 pad_maximum_fusion.1
  181.4 9.1 %copy.68 = f32[2,16,64,512]{2,1,0,3:T(8,128)} copy(f32[2,16,64,512]{3,2,1,0:T(8,128)} %pad_maximum_fusion.1) | data formatting | bytes 8388608
  190.5 7.6 pad.9.clone
  198.1 11.4 %all-to-all-start.1 = ((f32[2,16,128,512]{2,1,0,3:T(8,128)}), f32[2,16,128,512]{2,1,0,3:T(8,128)}, u32[]{:S(2)}, u32[]{:S(2)}) async-start(f32[2,16,128,512]{2,1,0,3:T(8,128)} %pad.9.clone), calls=%async_computation.1 | async-start | bytes 16777216 | tf_op jit(solution)/shard_map/all_to_all | solution.py:100
  209.6 90.8 %all-to-all-done.1 = f32[2,16,128,512]{2,1,0,3:T(8,128)} async-done(((f32[2,16,128,512]{2,1,0,3:T(8,128)}), f32[2,16,128,512]{2,1,0,3:T(8,128)}, u32[]{:S(2)}, u32[]{:S(2)}) %all-to-all-start.1) | async-done | bytes 8388640 | tf_op jit(solution)/shard_map/all_to_all | solution.py:100
  300.4 12.0 %copy.73 = f32[2,16,128,4,128]{2,3,4,1,0:T(4,128)} copy(f32[2,16,128,4,128]{2,1,0,4,3:T(8,128)} %bitcast.17) | data formatting | bytes 16777216 | tf_op jit(solution)/shard_map/all_to_all | solution.py:100
  312.4 7.6 fusion.362
  320.1 5.5 squeeze.56
  325.6 14.8 %fusion.32 = f32[16,128,512]{2,1,0:T(8,128)} fusion(f32[16,512,128]{1,2,0:T(8,128)} %squeeze.56, s32[512]{0:T(512)S(1)} %fusion.208), kind=kOutput, calls=%fused_computation.69 | convolution fusion | flops 6446383104 | bytes 8390656 | tf_op jit(solution)/shard_map/xzy,zq->xyq/dot_general | solution.py:61
  340.4 12.3 %fusion.36 = f32[16,128,512]{2,1,0:T(8,128)} fusion(f32[16,512,128]{1,2,0:T(8,128)S(1)} %copy-done.1, s32[512]{0:T(512)S(1)} %fusion.208), kind=kOutput, calls=%fused_computation.73 | convolution fusion | flops 6446120960 | bytes 8390656 | tf_op jit(solution)/shard_map/xzy,zq->xyq/dot_general | solution.py:58
  352.7 5.5 squeeze.57
  358.2 18.2 %convolution_add_fusion = f32[16,128,512]{2,1,0:T(8,128)S(1)} fusion(f32[16,128,512]{2,1,0:T(8,128)} %fusion.32, f32[16,512,128]{1,2,0:T(8,128)} %squeeze.57, s32[512]{0:T(512)S(1)} %fusion.208), kind=kOutput, calls=%fused_computation.13 | convolution fusion | flops 6447169536 | bytes 12584960 | tf_op jit(solution)/shard_map/xzy,zq->xyq/dot_general | solution.py:61
  376.4 17.9 %fusion.1 = (f32[16,128,512]{2,1,0:T(8,128)S(1)}, f32[16,128,512]{2,1,0:T(8,128)S(1)}) fusion(f32[16,128,512]{2,1,0:T(8,128)S(1)} %convolution_add_fusion, f32[2,16,128,512]{3,2,1,0:T(8,128)} %param.8, f32[16,128,512]{2,1,0:T(8,128)S(1)} %copy-done.2, f32[16,512,128]{1,2,0:T(8,128)S(1)} %copy-done, s32[512]{0:T(512)S(1)} %fusion.208), kind=kOutput, calls=%fused_computation.8 | convolution fusion | flops 6453723136 | bytes 29362176 | tf_op jit(solution)/shard_map/xzy,zq->xyq/dot_general | solution.py:58
  394.4 10.7 %fusion.30 = f32[16,128,512]{2,1,0:T(8,128)S(1)} fusion(f32[16,128,512]{2,1,0:T(8,128)S(1)} %get-tuple-element.4, s32[512]{0:T(512)S(1)} %fusion.208), kind=kOutput, calls=%fused_computation.67 | convolution fusion | flops 6446383104 | bytes 8390656 | tf_op jit(solution)/shard_map/xyq,qz->xyz/dot_general | solution.py:58
  405.0 10.9 %fusion.26 = f32[16,128,512]{2,1,0:T(8,128)S(1)} fusion(f32[16,128,512]{2,1,0:T(8,128)S(1)} %get-tuple-element.4, s32[512]{0:T(512)S(1)} %fusion.208), kind=kOutput, calls=%fused_computation.63 | convolution fusion | flops 6446383104 | bytes 8390656 | tf_op jit(solution)/shard_map/xyq,qz->xyz/dot_general | solution.py:61
  415.9 11.4 %subtract_bitcast_fusion = f32[1,16,128,512]{3,2,1,0:T(8,128)S(1)} fusion(f32[16,128,512]{2,1,0:T(8,128)S(1)} %fusion.30, f32[16,128,512]{2,1,0:T(8,128)S(1)} %get-tuple-element.3, s32[512]{0:T(512)S(1)} %fusion.208), kind=kOutput, calls=%fused_computation.12 | convolution fusion | flops 6447431680 | bytes 12584960 | tf_op jit(solution)/shard_map/xyq,qz->xyz/dot_general | solution.py:58
  427.4 11.4 %add_bitcast_fusion = f32[1,16,128,512]{3,2,1,0:T(8,128)S(1)} fusion(f32[16,128,512]{2,1,0:T(8,128)S(1)} %fusion.26, f32[16,128,512]{2,1,0:T(8,128)S(1)} %get-tuple-element.3, s32[512]{0:T(512)S(1)} %fusion.208), kind=kOutput, calls=%fused_computation.11 | convolution fusion | flops 6447431680 | bytes 12584960 | tf_op jit(solution)/shard_map/xyq,qz->xyz/dot_general | solution.py:61
  438.7 4.3 pad_maximum_fusion
  443.0 10.3 %copy.56 = f32[2,16,128,512]{2,1,0,3:T(8,128)} copy(f32[2,16,128,512]{3,2,1,0:T(8,128)} %pad_maximum_fusion) | data formatting | bytes 16777216 | tf_op jit(solution)/shard_map/stack | solution.py:64
  453.3 102.6 %all_to_all.66 = f32[2,16,128,512]{2,1,0,3:T(8,128)} all-to-all(f32[2,16,128,512]{2,1,0,3:T(8,128)} %copy.56), channel_id=1, replica_groups=mesh['gy'=32,'gz'=4] {'gz'}, dimensions={3} | all-to-all | bytes 16777216 | tf_op jit(solution)/shard_map/all_to_all | solution.py:109
  556.0 12.0 %copy.72 = f32[2,16,128,4,128]{2,3,4,1,0:T(4,128)} copy(f32[2,16,128,4,128]{2,1,0,4,3:T(8,128)} %bitcast.198) | data formatting | bytes 16777216 | tf_op jit(solution)/shard_map/all_to_all | solution.py:109
  568.0 10.3 %all_to_all.57 = f32[2,16,512,128]{2,3,1,0:T(8,128)} reshape(f32[2,16,4,128,128]{3,2,4,1,0:T(4,128)} %bitcast.199) | data formatting | bytes 16777216 | tf_op jit(solution)/shard_map/all_to_all | solution.py:109
  578.2 2.8 fusion.361
  581.0 8.4 %fusion.59 = f32[512,1024]{0,1:S(1)} fusion(f32[512,1024]{0,1:T(8,128)S(1)} %bitcast.213, s32[512]{0:T(512)S(1)} %fusion.204), kind=kOutput, calls=%fused_computation.102 | convolution fusion | flops 3225157632 | bytes 4196352
  589.4 8.8 %fusion.56 = f32[512,1024]{0,1:S(1)} fusion(f32[512,1024]{0,1:T(8,128)S(1)} %bitcast.214, s32[512]{0:T(512)S(1)} %fusion.204), kind=kOutput, calls=%fused_computation.99 | convolution fusion | flops 3225157632 | bytes 4196352
  598.2 8.4 %fusion.57 = f32[512,1024]{0,1:S(1)} fusion(f32[512,1024]{0,1:T(8,128)S(1)} %bitcast.209, s32[512]{0:T(512)S(1)} %fusion.204), kind=kOutput, calls=%fused_computation.100 | convolution fusion | flops 3225157632 | bytes 4196352
  606.6 8.5 %fusion.58 = f32[512,1024]{0,1:S(1)} fusion(f32[512,1024]{0,1:T(8,128)S(1)} %bitcast.210, s32[512]{0:T(512)S(1)} %fusion.204), kind=kOutput, calls=%fused_computation.101 | convolution fusion | flops 3225157632 | bytes 4196352
  616.5 2.4 pad_maximum_fusion.2
  618.9 9.1 %copy.58 = f32[2,512,64,16]{2,3,0,1:T(8,128)} copy(f32[2,512,64,16]{1,2,3,0:T(8,128)} %pad_maximum_fusion.2) | data formatting | bytes 8388608 | tf_op jit(solution)/shard_map/stack | solution.py:64
  628.0 9.8 %reshape.300 = f32[32,1,32768]{2,1,0:T(1,128)} reshape(f32[512,2,16,64]{3,2,1,0:T(8,128)} %bitcast.194) | data formatting | bytes 8388608
  637.8 5.0 all-to-all-start.3
  644.2 4.0 collective-permute-start
  649.6 24.7 %collective-permute-done = f32[4,256]{1,0:T(4,128)S(1)} collective-permute-done((f32[4,256]{1,0:T(4,128)S(1)}, f32[4,256]{1,0:T(4,128)S(1)}, u32[]{:S(2)}, u32[]{:S(2)}) %collective-permute-start) | collective-permute-done | bytes 4128 | tf_op jit(solution)/shard_map/ppermute | solution.py:27
  675.3 20.1 %all-to-all-done.3 = f32[32,1,32768]{2,1,0:T(1,128)} async-done(((f32[32,1,32768]{2,1,0:T(1,128)}), f32[32,1,32768]{2,1,0:T(1,128)}, u32[]{:S(2)}, u32[]{:S(2)}) %all-to-all-start.3) | async-done | bytes 4194336 | tf_op jit(solution)/shard_map/all_to_all | solution.py:115
  695.4 13.7 %reduce.1 = f32[32,32768]{1,0:T(8,128)} reduce(f32[32,1,32768]{2,1,0:T(1,128)} %all-to-all-done.3, f32[]{:T(128)} %broadcast.993), dimensions={1}, to_apply=%all_to_all.58.reduce_sub_computation | reduce | bytes 8388612 | tf_op jit(solution)/shard_map/all_to_all | solution.py:115
  709.2 7.6 reshape.301
  716.7 4.3 copy.60
  721.1 5.1 fusion.3
  726.2 5.1 fusion.2
  731.3 5.4 fusion.9
  736.7 5.1 fusion.11
  742.4 16.1 %psum.7 = f32[8,256]{1,0:T(8,128)S(1)} all-reduce(f32[8,256]{1,0:T(8,128)S(1)} %bitcast_multiply_fusion.4), channel_id=1, replica_groups=mesh['gy'=32,'gz'=4] {'gz'}, use_global_device_ids=true, to_apply=%region_1.2 | all-reduce | flops 2048 | bytes 16384 | tf_op jit(solution)/shard_map/psum | solution.py:125
  761.5 3.0 collective-permute-done.3
  (46 shorter events, 11.3 us)
Async XLA Ops:
  36.1 64.2 %all-to-all-start = ((f32[32,1,32768]{2,1,0:T(1,128)}), f32[32,1,32768]{2,1,0:T(1,128)}, u32[]{:S(2)}, u32[]{:S(2)}) async-start(f32[32,1,32768]{2,1,0:T(1,128)} %reshape.298), calls=%async_computation | async-start | bytes 8388608 | tf_op jit(solution)/shard_map/all_to_all | solution.py:91
  147.3 9.0 %copy-start.3 = (f32[1,32,16,64,16]{3,4,1,2,0:T(8,128)S(1)}, f32[1,32,16,64,16]{3,4,1,2,0:T(8,128)}, u32[]{:S(2)}) copy-start(f32[1,32,16,64,16]{3,4,1,2,0:T(8,128)} %get-tuple-element.9) | copy-start | bytes 6291460
  161.7 9.2 %copy-start.4 = (f32[512,64,16]{0,1,2:T(8,128)S(1)}, f32[512,64,16]{0,1,2:T(8,128)}, u32[]{:S(2)}) copy-start(f32[512,64,16]{0,1,2:T(8,128)} %fusion.38) | copy-start | bytes 6291460
  198.1 102.3 %all-to-all-start.1 = ((f32[2,16,128,512]{2,1,0,3:T(8,128)}), f32[2,16,128,512]{2,1,0,3:T(8,128)}, u32[]{:S(2)}, u32[]{:S(2)}) async-start(f32[2,16,128,512]{2,1,0,3:T(8,128)} %pad.9.clone), calls=%async_computation.1 | async-start | bytes 16777216 | tf_op jit(solution)/shard_map/all_to_all | solution.py:100
  325.6 14.8 %copy-start.1 = (f32[16,512,128]{1,2,0:T(8,128)S(1)}, f32[16,512,128]{1,2,0:T(8,128)}, u32[]{:S(2)}) copy-start(f32[16,512,128]{1,2,0:T(8,128)} %squeeze.56) | copy-start | bytes 12582916
  358.2 18.2 %copy-start = (f32[16,512,128]{1,2,0:T(8,128)S(1)}, f32[16,512,128]{1,2,0:T(8,128)}, u32[]{:S(2)}) copy-start(f32[16,512,128]{1,2,0:T(8,128)} %squeeze.57) | copy-start | bytes 12582916
  358.2 18.3 %copy-start.2 = (f32[16,128,512]{2,1,0:T(8,128)S(1)}, f32[16,128,512]{2,1,0:T(8,128)}, u32[]{:S(2)}) copy-start(f32[16,128,512]{2,1,0:T(8,128)} %fusion.36) | copy-start | bytes 12582916
  637.8 5.0 copy-start.8
  637.8 10.3 %copy-start.9 = (s32[2,16]{1,0:T(2,128)S(1)}, s32[2,16]{1,0:T(2,128)}, u32[]{:S(2)}) copy-start(s32[2,16]{1,0:T(2,128)} %param.11) | copy-start | bytes 388
  637.8 57.6 %all-to-all-start.3 = ((f32[32,1,32768]{2,1,0:T(1,128)}), f32[32,1,32768]{2,1,0:T(1,128)}, u32[]{:S(2)}, u32[]{:S(2)}) async-start(f32[32,1,32768]{2,1,0:T(1,128)} %reshape.300), calls=%async_computation.3 | async-start | bytes 8388608 | tf_op jit(solution)/shard_map/all_to_all | solution.py:115
  642.9 6.8 collective-permute-start.1
  644.2 30.1 %collective-permute-start = (f32[4,256]{1,0:T(4,128)S(1)}, f32[4,256]{1,0:T(4,128)S(1)}, u32[]{:S(2)}, u32[]{:S(2)}) collective-permute-start(f32[4,256]{1,0:T(4,128)S(1)} %get-tuple-element.14), channel_id=1, source_target_pairs={{0,4},{4,8},{8,12},{12,16},{16,20},{20,24},{24,28},{28,32},{32,36}... | collective-permute-start | bytes 12296 | tf_op jit(solution)/shard_map/ppermute | solution.py:27
  726.2 15.7 %copy-start.5 = (f32[2,8,64,256]{3,2,1,0:T(8,128)S(1)}, f32[2,8,64,256]{3,2,1,0:T(8,128)}, u32[]{:S(2)}) copy-start(f32[2,8,64,256]{3,2,1,0:T(8,128)} %param.6) | copy-start | bytes 3145732
  731.3 10.7 %copy-start.7 = (f32[2,8,64,256]{3,2,1,0:T(8,128)S(1)}, f32[2,8,64,256]{3,2,1,0:T(8,128)}, u32[]{:S(2)}) copy-start(f32[2,8,64,256]{3,2,1,0:T(8,128)} %param.9) | copy-start | bytes 3145732
  742.0 23.1 %copy-start.6 = (f32[2,8,64,256]{3,2,1,0:T(8,128)}, f32[2,8,64,256]{3,2,1,0:T(8,128)S(1)}, u32[]{:S(2)}) copy-start(f32[2,8,64,256]{3,2,1,0:T(8,128)S(1)} %maximum_subtract_fusion) | copy-start | bytes 3145732
  758.9 2.6 collective-permute-start.2
  760.1 4.4 collective-permute-start.3
where the time goes:
time: 780 us; the launch traced here: 766 us
  matrix products  212 us (27%)
  waiting for transfers between devices  192 us (25%)
  local copies, waits for them, and re-layouts  164 us (21%)
  blocking collectives  119 us (15%)
  other arithmetic  40.6 us (5%)
  starting transfers between devices  36 us (5%)
    all_to_all x1, blocking collectives, shards(): lax.all_to_all(spatial, 'gz', split_axis=3, concat_axis=2, tiled=True)  103 us
    all_to_all x1, waiting for transfers between devices, shards(): lax.all_to_all(spectral, 'gz', split_axis=3, concat_axis=2, tiled=True)  90.8 us
    unnamed x28, local copies, waits for them, and re-layouts  54.1 us
    all_to_all x1, waiting for transfers between devices, shards(): lax.all_to_all(spectral, 'gy', split_axis=3, concat_axis=1, tiled=True)  52.5 us
    dot_general x5, matrix products, complex_apply(): jnp.einsum(form, pair[1], sine, precision=highest)  47.4 us
    dot_general x5, matrix products, complex_apply(): jnp.einsum(form, pair[1], cosine, precision=highest)  46 us
    dot_general x5, matrix products, complex_apply(): jnp.einsum(form, pair[0], sine, precision=highest)  43.2 us
    dot_general x5, matrix products, complex_apply(): jnp.einsum(form, pair[0], cosine, precision=highest)  40.2 us
  transfers between devices with their start and end apart: 7, of which 6 were waited for; matrix products, arithmetic and copies ran while one was open for 0% of the time, Pallas kernels for 0%

commit v1 on v0

v1 whole, which is shorter than its diff:
```python
import functools

import jax
import jax.numpy as jnp
import ml_dtypes
import numpy as np
from jax import lax
from jax.experimental import pallas as pl
from jax.experimental.pallas import tpu as pltpu
from jax.sharding import PartitionSpec as P

NX = NY = NZ = 256
PAD = 512
SLAB = 32
RADIUS = 4
TILE_Y = 4
TILE_X = 16
Z0 = 112
SHARP = 8.0
GAP = 11.0

GY = 32
GZ = 4
ROWS = NY // GY
DEPTH = NZ // GZ
XF = PAD // GY
YF = PAD // GZ
LANES = 2 * DEPTH
CH = 4
CX = XF // CH

F32 = jnp.float32
BF16 = jnp.bfloat16
MESH = pl.DeviceIdType.MESH


def halves(table):
    high = table.astype(ml_dtypes.bfloat16)
    low = (table - high.astype(np.float64)).astype(ml_dtypes.bfloat16)
    return high, low


def tables():
    k = np.arange(PAD)[:, None]
    p = np.arange(NX)[None, :]
    angle = (k * p % PAD) * (2.0 * np.pi / PAD)
    cos, sin = np.cos(angle), np.sin(angle)
    order = np.arange(PAD).reshape(GY, CH, CX).transpose(1, 0, 2).reshape(CH, GY * CX)
    fx = np.concatenate([cos[order], sin[order]], axis=2)
    fy = np.concatenate([cos, sin], axis=1).reshape(GZ, YF, 2 * NY)
    fyi = np.concatenate([cos.T, -sin.T], axis=1)
    fxi = np.concatenate(
        [cos[order].transpose(0, 2, 1), -sin[order].transpose(0, 2, 1)], axis=2
    )
    c4 = cos.reshape(2, 256, GZ, DEPTH)
    s4 = sin.reshape(2, 256, GZ, DEPTH)
    ct, st = c4.transpose(0, 2, 3, 1), s4.transpose(0, 2, 3, 1)
    re_rows = np.concatenate([ct, -st], axis=3)
    im_rows = np.concatenate([st, ct], axis=3)
    wz = np.stack([re_rows, im_rows], axis=2).reshape(2, 2 * NZ, 512)
    wzi = wz.transpose(0, 2, 1).reshape(1024, 512)
    flat = []
    for table in (fx, fy, fyi, fxi, wz, wzi):
        flat.extend(halves(table))
    cells = np.arange(NX)
    tent = np.maximum(RADIUS + 1 - np.abs(cells[:, None] - cells[None, :]), 0).astype(
        np.float32
    )
    filt = tent / tent.sum(axis=1, keepdims=True)
    return flat + [filt, np.ascontiguousarray(filt.T)]


def split(value):
    high = value.astype(BF16)
    return high, (value - high.astype(F32)).astype(BF16)


def product(ah, al, bh, bl):
    dot = functools.partial(jnp.dot, preferred_element_type=F32)
    return dot(ah, bh) + dot(al, bh) + dot(ah, bl)


def turned(block, sign):
    return pltpu.roll(block, DEPTH, 1) * sign


def turned_pair(pair, sign):
    return jnp.concatenate(
        [turned(pair[:, :LANES], sign), turned(pair[:, LANES:], sign)], axis=1
    )


def kernel(*refs):
    (src_h, con_h, fwd_h, green_h, dens, level) = refs[:6]
    tabs_h = refs[6:20]
    adj, proj, grad = refs[20:23]
    (src, con, fwd, green) = refs[23:27]
    tabs = refs[27:41]
    (sth, stl, s1, r1, y1, r2, zi, r3, yi, r4, acc, bh, bl, ah, al, qh, ql) = refs[41:58]
    (near, fact, slab, slabs) = refs[58:62]
    (in_sem, tab_sem, ss1, rs1, ls1, ss2, rs2, ls2) = refs[62:70]
    (ss3, rs3, ls3, ss4, rs4, ls4, sn, rn, sf, rf, sp, rp) = refs[70:82]
    fxh, fxl, fyh, fyl, fyih, fyil, fxih, fxil, wzh, wzl, wih, wil, filt, filt_t = tabs

    me = lax.axis_index("gy")
    mz = lax.axis_index("gz")
    after, before = lax.rem(me + 1, GY), lax.rem(me + GY - 1, GY)

    slab_z = pl.multiple_of(jnp.where(mz == 1, 48, 0), 16)
    loads = [
        pltpu.make_async_copy(src_h, src, in_sem.at[0]),
        pltpu.make_async_copy(con_h, con, in_sem.at[1]),
        pltpu.make_async_copy(fwd_h.at[:, :, pl.ds(slab_z, 16), :], fwd, in_sem.at[2]),
        pltpu.make_async_copy(green_h, green, in_sem.at[3]),
    ]
    fills = [
        pltpu.make_async_copy(tabs_h[n], tabs[n], tab_sem.at[n]) for n in range(14)
    ]
    loads[0].start()
    loads[1].start()
    for n in range(12):
        fills[n].start()
    loads[3].start()
    fills[12].start()
    fills[13].start()
    loads[2].start()

    barrier = pltpu.get_barrier_semaphore()

    @pl.loop(1, GY)
    def _(k):
        pl.semaphore_signal(
            barrier, inc=1, device_id={"gy": lax.rem(me + k, GY)}, device_id_type=MESH
        )

    for k in range(1, GZ):
        other = lax.rem(mz + k, GZ)
        pl.semaphore_signal(barrier, inc=1, device_id={"gz": other}, device_id_type=MESH)
        for row in (after, before):
            pl.semaphore_signal(
                barrier,
                inc=1,
                device_id={"gy": row, "gz": other},
                device_id_type=MESH,
            )

    lane = lax.broadcasted_iota(jnp.int32, (1, LANES), 1)
    sign = jnp.where(lane < DEPTH, 1.0, -1.0).astype(F32)

    loads[0].wait()
    loads[1].wait()

    @pl.loop(0, ROWS)
    def _(y):
        weight = con[y]
        both = jnp.concatenate([src[0, y] * weight, src[1, y] * weight], axis=0)
        flat = both.T
        full = jnp.concatenate([flat, turned(flat, sign)], axis=0)
        high, low = split(full)
        sth[y] = high
        stl[y] = low

    fills[0].wait()
    fills[1].wait()

    pl.semaphore_wait(barrier, (GY - 1) + 3 * (GZ - 1))

    def near_copy(buffer, slot, target, sems, recv):
        return pltpu.make_async_remote_copy(
            src_ref=buffer.at[2],
            dst_ref=buffer.at[slot],
            send_sem=sems.at[slot],
            recv_sem=recv.at[slot],
            device_id={"gy": target},
            device_id_type=MESH,
        )

    near[2] = dens[...]
    near_copies = [near_copy(near, 0, after, sn, rn), near_copy(near, 1, before, sn, rn)]
    for copy in near_copies:
        copy.start()

    @pl.loop(0, CH)
    def _(i):
        lh, ll = fxh[i], fxl[i]
        for k in range(ROWS // 2):
            rh = jnp.concatenate([sth[2 * k], sth[2 * k + 1]], axis=1)
            rl = jnp.concatenate([stl[2 * k], stl[2 * k + 1]], axis=1)
            out = product(lh, ll, rh, rl)
            s1[i, :, 2 * k, :] = out[:, :LANES]
            s1[i, :, 2 * k + 1, :] = out[:, LANES:]

        def part(p):
            return s1.at[i, pl.ds(CX * p, CX)]

        mine = r1.at[pl.ds(CX * i, CX), pl.ds(pl.multiple_of(ROWS * me, ROWS), ROWS), :]

        @pl.loop(1, GY)
        def _(k):
            p = lax.rem(me + k, GY)
            pltpu.make_async_remote_copy(
                src_ref=part(p),
                dst_ref=mine,
                send_sem=ss1.at[i],
                recv_sem=rs1.at[i],
                device_id={"gy": p},
                device_id_type=MESH,
            ).start()

        pltpu.make_async_copy(part(me), mine, ls1.at[i]).start()

    fills[12].wait()
    fills[13].wait()
    for copy in near_copies:
        copy.wait()

    def wide(buffer):
        rows = jnp.concatenate(
            [buffer[0][ROWS - RADIUS :], buffer[2], buffer[1][:RADIUS]], axis=0
        )
        return jnp.where(inside, rows, 0.0)

    row = ROWS * me - RADIUS + lax.broadcasted_iota(jnp.int32, (2 * ROWS, NX), 0)
    inside = (row >= 0) & (row < NY)
    weight16 = jnp.zeros((2 * ROWS, NX), F32)
    for offset in range(-RADIUS, RADIUS + 1):
        valid = (row + offset >= 0) & (row + offset < NY)
        weight16 = weight16 + jnp.where(valid, float(RADIUS + 1 - abs(offset)), 0.0)

    def tent_rows(rows):
        total = jnp.zeros((ROWS, NX), F32)
        for offset in range(-RADIUS, RADIUS + 1):
            start = RADIUS + offset
            total = total + float(RADIUS + 1 - abs(offset)) * rows[start : start + ROWS]
        return total

    exact = functools.partial(
        jnp.dot, preferred_element_type=F32, precision=lax.Precision.HIGHEST
    )
    smooth = tent_rows(wide(near)) / weight16[RADIUS : RADIUS + ROWS]
    filtered = exact(smooth, filt_t[...])
    threshold = level[...]
    steep = jnp.tanh(SHARP * (filtered - threshold))
    shift = jnp.tanh(SHARP * threshold)
    below = shift + jnp.tanh(SHARP * (1.0 - threshold))
    proj[...] = (shift + steep) / below
    fact[2] = SHARP * (1.0 - steep * steep) / below
    fact_copies = [near_copy(fact, 0, after, sf, rf), near_copy(fact, 1, before, sf, rf)]
    for copy in fact_copies:
        copy.start()

    for n in range(2, 12):
        fills[n].wait()
    loads[3].wait()

    @pl.loop(0, CH)
    def _(i):
        rows = pl.ds(CX * i, CX)
        got = r1.at[rows, pl.ds(0, NY - ROWS), :]
        pltpu.make_async_copy(got, got, rs1.at[i]).wait()
        own = r1.at[rows, pl.ds(0, ROWS), :]
        pltpu.make_async_copy(own, own, ls1.at[i]).wait()

        @pl.loop(0, CX // 2)
        def _(k):
            x = CX * i + 2 * k
            pair = jnp.concatenate([r1[x], r1[x + 1]], axis=1)
            full = jnp.concatenate([pair, turned_pair(pair, sign)], axis=0)
            high, low = split(full)
            bh[: 2 * NY] = high
            bl[: 2 * NY] = low
            for d in range(GZ):
                out = product(fyh[d], fyl[d], bh[: 2 * NY], bl[: 2 * NY])
                y1[x, d * YF : (d + 1) * YF, :] = out[:, :LANES]
                y1[x + 1, d * YF : (d + 1) * YF, :] = out[:, LANES:]

        def part(d):
            return y1.at[rows, pl.ds(pl.multiple_of(YF * d, YF), YF), :]

        for k in range(1, GZ):
            d = lax.rem(mz + k, GZ)
            pltpu.make_async_remote_copy(
                src_ref=part(d),
                dst_ref=r2.at[mz, rows],
                send_sem=ss2.at[i],
                recv_sem=rs2.at[i],
                device_id={"gz": d},
                device_id_type=MESH,
            ).start()
        pltpu.make_async_copy(part(mz), r2.at[mz, rows], ls2.at[i]).start()

    @pl.loop(0, CH)
    def _(i):
        rows = pl.ds(CX * i, CX)
        got = r2.at[pl.ds(0, GZ - 1), rows]
        pltpu.make_async_copy(got, got, rs2.at[i]).wait()
        own = r2.at[0, rows]
        pltpu.make_async_copy(own, own, ls2.at[i]).wait()

        @pl.loop(0, CX // 2)
        def _(k):
            x = CX * i + 2 * k
            for j in range(2):
                line = jnp.concatenate([r2[d, x + j] for d in range(GZ)], axis=1)
                high, low = split(line)
                ah[j * YF : (j + 1) * YF] = high
                al[j * YF : (j + 1) * YF] = low
            for n in range(2):
                out = product(ah[...], al[...], wzh[n], wzl[n])
                for j in range(2):
                    lines = slice(j * YF, (j + 1) * YF)
                    real, imag = out[lines, :256], out[lines, 256:]
                    g_real = green[0, x + j, :, 256 * n : 256 * n + 256]
                    g_imag = green[1, x + j, :, 256 * n : 256 * n + 256]
                    high, low = split(real * g_real - imag * g_imag)
                    qh[lines, 512 * n : 512 * n + 256] = high
                    ql[lines, 512 * n : 512 * n + 256] = low
                    high, low = split(real * g_imag + imag * g_real)
                    qh[lines, 512 * n + 256 : 512 * n + 512] = high
                    ql[lines, 512 * n + 256 : 512 * n + 512] = low
            out = product(qh[...], ql[...], wih[...], wil[...])
            for j in range(2):
                for d in range(GZ):
                    zi[d, x + j] = out[j * YF : (j + 1) * YF, d * LANES : (d + 1) * LANES]

        mine = r3.at[rows, pl.ds(pl.multiple_of(YF * mz, YF), YF), :]
        for k in range(1, GZ):
            d = lax.rem(mz + k, GZ)
            pltpu.make_async_remote_copy(
                src_ref=zi.at[d, rows],
                dst_ref=mine,
                send_sem=ss3.at[i],
                recv_sem=rs3.at[i],
                device_id={"gz": d},
                device_id_type=MESH,
            ).start()
        pltpu.make_async_copy(zi.at[mz, rows], mine, ls3.at[i]).start()

    @pl.loop(0, CH)
    def _(i):
        rows = pl.ds(CX * i, CX)
        got = r3.at[rows, pl.ds(0, PAD - YF), :]
        pltpu.make_async_copy(got, got, rs3.at[i]).wait()
        own = r3.at[rows, pl.ds(0, YF), :]
        pltpu.make_async_copy(own, own, ls3.at[i]).wait()

        @pl.loop(0, CX // 2)
        def _(k):
            x = CX * i + 2 * k
            pair = jnp.concatenate([r3[x], r3[x + 1]], axis=1)
            full = jnp.concatenate([pair, turned_pair(pair, sign)], axis=0)
            high, low = split(full)
            bh[...] = high
            bl[...] = low
            out = product(fyih[...], fyil[...], bh[...], bl[...])
            yi[x] = out[:, :LANES]
            yi[x + 1] = out[:, LANES:]

        def part(p):
            return yi.at[rows, pl.ds(pl.multiple_of(ROWS * p, ROWS), ROWS), :]

        mine = r4.at[i, pl.ds(CX * me, CX)]

        @pl.loop(1, GY)
        def _(k):
            p = lax.rem(me + k, GY)
            pltpu.make_async_remote_copy(
                src_ref=part(p),
                dst_ref=mine,
                send_sem=ss4.at[i],
                recv_sem=rs4.at[i],
                device_id={"gy": p},
                device_id_type=MESH,
            ).start()

        pltpu.make_async_copy(part(me), mine, ls4.at[i]).start()

    acc[...] = jnp.zeros_like(acc)

    @pl.loop(0, CH)
    def _(i):
        got = r4.at[i, pl.ds(0, CX * (GY - 1))]
        pltpu.make_async_copy(got, got, rs4.at[i]).wait()
        own = r4.at[i, pl.ds(0, CX)]
        pltpu.make_async_copy(own, own, ls4.at[i]).wait()
        lh, ll = fxih[i], fxil[i]
        for k in range(ROWS // 2):
            pair = jnp.concatenate([r4[i, :, 2 * k, :], r4[i, :, 2 * k + 1, :]], axis=1)
            full = jnp.concatenate([pair, turned_pair(pair, sign)], axis=0)
            high, low = split(full)
            acc[k] += product(lh, ll, high, low)

    scale = 1.0 / float(PAD) ** 3

    @pl.loop(0, ROWS // 2)
    def _(k):
        for j in range(2):
            flat = acc[k, :, j * LANES : (j + 1) * LANES].T * scale
            adj[0, 2 * k + j] = src[0, 2 * k + j] - flat[:DEPTH]
            adj[1, 2 * k + j] = src[1, 2 * k + j] - flat[DEPTH:]

    loads[2].wait()
    holds = (mz == 1) | (mz == 2)
    slot = jnp.where(mz == 2, 1, 0)

    def slab_copy(step, turn):
        return pltpu.make_async_remote_copy(
            src_ref=slab,
            dst_ref=slabs.at[1 - step, slot],
            send_sem=sp.at[step + 1, turn],
            recv_sem=rp.at[1 - step, slot],
            device_id={
                "gy": lax.rem(me + GY + step, GY),
                "gz": lax.rem(mz + turn, GZ),
            },
            device_id_type=MESH,
        )

    reaches = [
        (step, turn) for step in (-1, 0, 1) for turn in range(GZ) if step or turn
    ]

    @pl.when(holds)
    def _():
        planes = pl.ds(slab_z, 16)
        field = adj[0, :, planes, :] * fwd[0] - adj[1, :, planes, :] * fwd[1]
        total = jnp.sum(field, axis=1) * (GAP / SLAB)
        slab[...] = total
        slabs[1, slot] = total
        for step, turn in reaches:
            slab_copy(step, turn).start()

    for copy in fact_copies:
        copy.wait()
    for step in range(3):
        for source in range(2):
            arrived = pltpu.make_async_copy(slab, slabs.at[step, source], rp.at[step, source])
            if step == 1:

                @pl.when(mz != source + 1)
                def _(arrived=arrived):
                    arrived.wait()

            else:
                arrived.wait()

    summed = [slabs[step, 0] + slabs[step, 1] for step in range(3)]
    sense = jnp.concatenate(
        [summed[0][ROWS - RADIUS :], summed[1], summed[2][:RADIUS]], axis=0
    )
    weighted = jnp.where(inside, wide(fact) * sense, 0.0)
    scaled = exact(weighted, filt[...]) / jnp.where(inside, weight16, 1.0)
    grad[...] = tent_rows(scaled)

    @pl.when(holds)
    def _():
        for step, turn in reaches:
            slab_copy(step, turn).wait_send()

    @pl.loop(0, CH)
    def _(i):
        rows = pl.ds(CX * i, CX)
        sent = s1.at[i, pl.ds(0, CX * (GY - 1))]
        pltpu.make_async_copy(sent, sent, ss1.at[i]).wait()
        sent = r2.at[pl.ds(0, GZ - 1), rows]
        pltpu.make_async_copy(sent, sent, ss2.at[i]).wait()
        sent = zi.at[pl.ds(0, GZ - 1), rows]
        pltpu.make_async_copy(sent, sent, ss3.at[i]).wait()
        sent = yi.at[rows, pl.ds(0, NY - ROWS), :]
        pltpu.make_async_copy(sent, sent, ss4.at[i]).wait()


def shards(source, contrast, green, forward_field, density, thresh_index):
    levels = 0.35 + 0.1 * thresh_index.astype(F32)
    threshold = jnp.broadcast_to(
        levels[:, None, :, None], (levels.shape[0], TILE_Y, levels.shape[1], TILE_X)
    ).reshape(ROWS, NX)
    constants = tables()
    anywhere = pl.BlockSpec(memory_space=pl.ANY)
    vmem = pl.BlockSpec(memory_space=pltpu.VMEM)
    dma = pltpu.SemaphoreType.DMA
    block = pltpu.VMEM
    scratch = [
        block((2, ROWS, DEPTH, NX), F32),
        block((ROWS, DEPTH, NX), F32),
        block((2, ROWS, 16, NX), F32),
        block((2, XF, YF, PAD), F32),
    ]
    scratch += [block(table.shape, table.dtype) for table in constants]
    scratch += [
        block((ROWS, 2 * NX, LANES), BF16),
        block((ROWS, 2 * NX, LANES), BF16),
        block((CH, GY * CX, ROWS, LANES), F32),
        block((XF, NY, LANES), F32),
        block((XF, PAD, LANES), F32),
        block((GZ, XF, YF, LANES), F32),
        block((GZ, XF, YF, LANES), F32),
        block((XF, PAD, LANES), F32),
        block((XF, NY, LANES), F32),
        block((CH, GY * CX, ROWS, LANES), F32),
        block((ROWS // 2, NX, 2 * LANES), F32),
        block((2 * PAD, 2 * LANES), BF16),
        block((2 * PAD, 2 * LANES), BF16),
        block((2 * YF, 2 * NZ), BF16),
        block((2 * YF, 2 * NZ), BF16),
        block((2 * YF, 2 * PAD), BF16),
        block((2 * YF, 2 * PAD), BF16),
        block((3, ROWS, NX), F32),
        block((3, ROWS, NX), F32),
        block((ROWS, NX), F32),
        block((3, 2, ROWS, NX), F32),
        dma((4,)),
        dma((14,)),
    ]
    scratch += [dma((CH,)) for _ in range(12)]
    scratch += [dma((2,)) for _ in range(4)]
    scratch += [dma((3, GZ)), dma((3, 2))]
    return pl.pallas_call(
        kernel,
        out_shape=(
            jax.ShapeDtypeStruct((2, ROWS, DEPTH, NX), F32),
            jax.ShapeDtypeStruct((ROWS, NX), F32),
            jax.ShapeDtypeStruct((ROWS, NX), F32),
        ),
        in_specs=[anywhere] * 4 + [vmem] * 2 + [anywhere] * 14,
        out_specs=(vmem, vmem, vmem),
        scratch_shapes=scratch,
        compiler_params=pltpu.CompilerParams(
            collective_id=0, has_side_effects=True, vmem_limit_bytes=62 << 20
        ),
    )(source, contrast, forward_field, green, density, threshold, *map(jnp.asarray, constants))


def solution(mesh):
    return jax.shard_map(
        shards,
        mesh=mesh,
        in_specs=(
            P(None, "gy", "gz", None),
            P("gy", "gz", None),
            P(None, "gy", "gz", None),
            P(None, "gy", "gz", None),
            P("gy", None),
            P("gy", None),
        ),
        out_specs=(P(None, "gy", "gz", None), P("gy", None), P("gy", None)),
        check_vma=False,
    )
```

time: 780 us -> 168 us (0.22); the launches traced: 766 us -> 168 us
  matrix products: 212 us -> 0 us
  waiting for transfers between devices: 192 us -> 0 us
  Pallas kernels: 0 us -> 161 us
  local copies, waits for them, and re-layouts: 164 us -> 5.65 us
  blocking collectives: 119 us -> 0 us
  other arithmetic: 40.6 us -> 0.68 us
  starting transfers between devices: 36 us -> 0 us
    dot_general x23 -> x0, matrix products: 178 us -> none  [the longest x5 47.4 us: complex_apply(): jnp.einsum(form, pair[1], sine, precision=highest)]
    all_to_all x3 -> x0, waiting for transfers between devices: 163 us -> none  [the longest x1 90.8 us: shards(): lax.all_to_all(spectral, 'gz', split_axis=3, concat_axis=2, tiled=True)]
    pallas_call x0 -> x1, Pallas kernels: none -> 161 us  [shards(): pl.pallas_call(kernel, out_shape=(jax.ShapeDtypeStruct((2, ROWS, DEPTH, N...]
    all_to_all x1 -> x0, blocking collectives: 103 us -> none  [shards(): lax.all_to_all(spatial, 'gz', split_axis=3, concat_axis=2, tiled=True)]
    unnamed x28 -> x3, local copies, waits for them, and re-layouts: 54.1 us -> 4.88 us
    all_to_all x6 -> x0, local copies, waits for them, and re-layouts: 47.4 us -> none  [the longest x2 22.3 us: shards(): lax.all_to_all(spatial, 'gz', split_axis=3, concat_axis=2, tiled=True)]
    unnamed x4 -> x0, matrix products: 34 us -> none
    ppermute x4 -> x0, waiting for transfers between devices: 28.8 us -> none  [the longest x2 24.7 us: extended(): lax.ppermute(lax.slice_in_dim(block, block.shape[dim] - width, None, axis...]
  transfers between devices with their start and end apart: 7 -> 0, of which waited for: 6 -> 0; matrix products, arithmetic and copies ran while one was open for 0% -> 0% of each run, Pallas kernels for 0% -> 0%
where the time goes in v1:
time: 168 us
  Pallas kernels  161 us (96%)
  local copies, waits for them, and re-layouts  5.65 us (3%)
    pallas_call x1, Pallas kernels, shards(): pl.pallas_call(kernel, out_shape=(jax.ShapeDtypeStruct((2, ROWS, DEPTH, N...  161 us
    unnamed x3, local copies, waits for them, and re-layouts  4.88 us

profile of v1, /device:TPU:1, one launch (start us, length us, event | category | flops | bytes accessed | tf_op | source)
XLA Modules:
  0.0 167.9 jit_solution(6706292158066757684)
XLA Ops:
  0.6 0.7 multiply_add_fusion
  1.3 0.1 broadcast_in_dim.2
  1.4 0.7 reshape.10.refs_5_
  2.1 160.9 %shard_map.211 = (f32[2,8,64,256]{3,2,1,0:T(8,128)}, f32[8,256]{1,0:T(8,128)}, f32[8,256]{1,0:T(8,128)}) custom-call(f32[2,8,64,256]{3,2,1,0:T(8,128)} %refs_0_.1, f32[8,64,256]{2,1,0:T(8,128)} %refs_1_.1, f32[2,8,64,256]{3,2,1,0:T(8,128)} %refs_2_.1, f32[2,16,128,512]{3,2,1,0:T(8,128)} %refs_3_.1, f32[8,256]{1,0:T(8,128)} %refs_4_.1, ...), custom_call_target="tpu_custom_call" | custom-call | tf_op jit(solution)/shard_map/pallas_call | solution.py:518
  163.0 2.3 %copy.26 = f32[2,8,64,256]{3,2,1,0:T(8,128)} copy(f32[2,8,64,256]{3,2,1,0:T(8,128)} %get-tuple-element.6) | data formatting | bytes 2097152
  165.3 1.3 copy.27
  166.6 1.3 copy.28

commit v2 on v1

--- a/solution.py
+++ b/solution.py
@@ -48,16 +48,20 @@
     order = np.arange(PAD).reshape(GY, CH, CX).transpose(1, 0, 2).reshape(CH, GY * CX)
     fx = np.concatenate([cos[order], sin[order]], axis=2)
     fy = np.concatenate([cos, sin], axis=1).reshape(GZ, YF, 2 * NY)
-    fyi = np.concatenate([cos.T, -sin.T], axis=1)
+    half = (2, PAD // 2, NY)
+    fyi = np.concatenate(
+        [cos.reshape(half).transpose(0, 2, 1), -sin.reshape(half).transpose(0, 2, 1)],
+        axis=2,
+    )
     fxi = np.concatenate(
         [cos[order].transpose(0, 2, 1), -sin[order].transpose(0, 2, 1)], axis=2
     )
-    c4 = cos.reshape(2, 256, GZ, DEPTH)
-    s4 = sin.reshape(2, 256, GZ, DEPTH)
-    ct, st = c4.transpose(0, 2, 3, 1), s4.transpose(0, 2, 3, 1)
-    re_rows = np.concatenate([ct, -st], axis=3)
-    im_rows = np.concatenate([st, ct], axis=3)
-    wz = np.stack([re_rows, im_rows], axis=2).reshape(2, 2 * NZ, 512)
+    shape = (2, 256, 2, 2, DEPTH)
+    ct = cos.reshape(shape).transpose(0, 3, 2, 4, 1)
+    st = sin.reshape(shape).transpose(0, 3, 2, 4, 1)
+    re_rows = np.concatenate([ct, -st], axis=4)
+    im_rows = np.concatenate([st, ct], axis=4)
+    wz = np.stack([re_rows, im_rows], axis=3).reshape(2, 2 * NZ, 512)
     wzi = wz.transpose(0, 2, 1).reshape(1024, 512)
     flat = []
     for table in (fx, fy, fyi, fxi, wz, wzi):
@@ -96,15 +100,26 @@
     adj, proj, grad = refs[20:23]
     (src, con, fwd, green) = refs[23:27]
     tabs = refs[27:41]
-    (sth, stl, s1, r1, y1, r2, zi, r3, yi, r4, acc, bh, bl, ah, al, qh, ql) = refs[41:58]
-    (near, fact, slab, slabs) = refs[58:62]
-    (in_sem, tab_sem, ss1, rs1, ls1, ss2, rs2, ls2) = refs[62:70]
-    (ss3, rs3, ls3, ss4, rs4, ls4, sn, rn, sf, rf, sp, rp) = refs[70:82]
+    (sth, stl, s1, r1, y1, r2, zi, r3, yp, yr, yi, r4, acc) = refs[41:54]
+    (bh, bl, ah, al, qh, ql, near, fact, slab, slabs) = refs[54:64]
+    (in_sem, tab_sem, sn, rn, sf, rf, sp, rp) = refs[64:72]
+    (ss1, rs1, ss2, rs2, ss3, rs3, ls3, ss4, rs4, ls4, ss5, rs5, ss6, rs6) = refs[72:86]
     fxh, fxl, fyh, fyl, fyih, fyil, fxih, fxil, wzh, wzl, wih, wil, filt, filt_t = tabs
 
     me = lax.axis_index("gy")
     mz = lax.axis_index("gz")
     after, before = lax.rem(me + 1, GY), lax.rem(me + GY - 1, GY)
+    core, chip = lax.rem(mz, 2), mz // 2
+    side = lax.rem(me // 4, 2)
+    sibling = mz + 1 - 2 * core
+    partner = lax.rem(mz + 2, GZ)
+
+    def place(p):
+        return p // 8, lax.rem(p // 4, 2), pl.multiple_of(ROWS * lax.rem(p, 4), ROWS)
+
+    def across(p):
+        same = lax.rem(p // 4, 2) == side
+        return {"gy": p, "gz": jnp.where(same, mz, partner)}
 
     slab_z = pl.multiple_of(jnp.where(mz == 1, 48, 0), 16)
     loads = [
@@ -130,13 +145,12 @@
     @pl.loop(1, GY)
     def _(k):
         pl.semaphore_signal(
-            barrier, inc=1, device_id={"gy": lax.rem(me + k, GY)}, device_id_type=MESH
+            barrier, inc=1, device_id=across(lax.rem(me + k, GY)), device_id_type=MESH
         )
 
-    for k in range(1, GZ):
+    for k in range(GZ):
         other = lax.rem(mz + k, GZ)
-        pl.semaphore_signal(barrier, inc=1, device_id={"gz": other}, device_id_type=MESH)
-        for row in (after, before):
+        for row in (after, before) + ((me,) if k else ()):
             pl.semaphore_signal(
                 barrier,
                 inc=1,
@@ -163,7 +177,7 @@
     fills[0].wait()
     fills[1].wait()
 
-    pl.semaphore_wait(barrier, (GY - 1) + 3 * (GZ - 1))
+    pl.semaphore_wait(barrier, (GY - 1) + 2 * GZ + (GZ - 1))
 
     def near_copy(buffer, slot, target, sems, recv):
         return pltpu.make_async_remote_copy(
@@ -193,7 +207,8 @@
         def part(p):
             return s1.at[i, pl.ds(CX * p, CX)]
 
-        mine = r1.at[pl.ds(CX * i, CX), pl.ds(pl.multiple_of(ROWS * me, ROWS), ROWS), :]
+        group, pair, first = place(me)
+        mine = r1.at[chip, pl.ds(CX * i, CX), group, pair, pl.ds(first, ROWS)]
 
         @pl.loop(1, GY)
         def _(k):
@@ -203,11 +218,11 @@
                 dst_ref=mine,
                 send_sem=ss1.at[i],
                 recv_sem=rs1.at[i],
-                device_id={"gy": p},
+                device_id=across(p),
                 device_id_type=MESH,
             ).start()
 
-        pltpu.make_async_copy(part(me), mine, ls1.at[i]).start()
+        pltpu.make_async_copy(part(me), mine, rs1.at[i]).start()
 
     fills[12].wait()
     fills[13].wait()
@@ -249,59 +264,91 @@
     for copy in fact_copies:
         copy.start()
 
+    def swap(source, target, i, sends, recvs):
+        return [
+            pltpu.make_async_remote_copy(
+                src_ref=source[n],
+                dst_ref=target[n],
+                send_sem=sends.at[i, n],
+                recv_sem=recvs.at[i, n],
+                device_id={"gz": partner},
+                device_id_type=MESH,
+            )
+            for n in range(2)
+        ]
+
+    def gathered(i):
+        rows = pl.ds(CX * i, CX)
+        pieces = [r1.at[chip, rows, :, side], r1.at[1 - chip, rows, :, 1 - side]]
+        return swap(pieces, pieces, i, ss2, rs2)
+
+    def to_sibling(source, target, i, send, recv):
+        return pltpu.make_async_remote_copy(
+            src_ref=source,
+            dst_ref=target,
+            send_sem=send.at[i],
+            recv_sem=recv.at[i],
+            device_id={"gz": sibling},
+            device_id_type=MESH,
+        )
+
+    def quarters(i):
+        rows = pl.ds(CX * i, CX)
+        away = to_sibling(y1.at[1 - core, rows], r2.at[core, rows], i, ss3, rs3)
+        return away, pltpu.make_async_copy(y1.at[core, rows], r2.at[core, rows], ls3.at[i])
+
+    def blocks(i):
+        rows = pl.ds(CX * i, CX)
+        mine = r3.at[rows, pl.ds(pl.multiple_of(YF * core, YF), YF), :]
+        away = to_sibling(zi.at[1 - core, rows], mine, i, ss4, rs4)
+        return away, pltpu.make_async_copy(zi.at[core, rows], mine, ls4.at[i])
+
+    def partials(i):
+        rows = pl.ds(CX * i, CX)
+        pieces = [yp.at[1 - chip, rows, :, side], yp.at[chip, rows, :, 1 - side]]
+        return swap(pieces, [yr.at[n, rows] for n in range(2)], i, ss5, rs5)
+
+    @pl.loop(0, CH)
+    def _(i):
+        whole = r1.at[0, pl.ds(CX * i, CX)]
+        pltpu.make_async_copy(whole, whole, rs1.at[i]).wait()
+        for copy in gathered(i):
+            copy.start()
+
     for n in range(2, 12):
         fills[n].wait()
     loads[3].wait()
 
     @pl.loop(0, CH)
     def _(i):
-        rows = pl.ds(CX * i, CX)
-        got = r1.at[rows, pl.ds(0, NY - ROWS), :]
-        pltpu.make_async_copy(got, got, rs1.at[i]).wait()
-        own = r1.at[rows, pl.ds(0, ROWS), :]
-        pltpu.make_async_copy(own, own, ls1.at[i]).wait()
-
-        @pl.loop(0, CX // 2)
+        for copy in gathered(i):
+            copy.wait_recv()
+
+        @pl.loop(0, CX)
         def _(k):
-            x = CX * i + 2 * k
-            pair = jnp.concatenate([r1[x], r1[x + 1]], axis=1)
-            full = jnp.concatenate([pair, turned_pair(pair, sign)], axis=0)
+            x = CX * i + k
+            both = jnp.concatenate(
+                [r1[0, x].reshape(NY, LANES), r1[1, x].reshape(NY, LANES)], axis=1
+            )
+            full = jnp.concatenate([both, turned_pair(both, sign)], axis=0)
             high, low = split(full)
-            bh[: 2 * NY] = high
-            bl[: 2 * NY] = low
-            for d in range(GZ):
-                out = product(fyh[d], fyl[d], bh[: 2 * NY], bl[: 2 * NY])
-                y1[x, d * YF : (d + 1) * YF, :] = out[:, :LANES]
-                y1[x + 1, d * YF : (d + 1) * YF, :] = out[:, LANES:]
-
-        def part(d):
-            return y1.at[rows, pl.ds(pl.multiple_of(YF * d, YF), YF), :]
-
-        for k in range(1, GZ):
-            d = lax.rem(mz + k, GZ)
-            pltpu.make_async_remote_copy(
-                src_ref=part(d),
-                dst_ref=r2.at[mz, rows],
-                send_sem=ss2.at[i],
-                recv_sem=rs2.at[i],
-                device_id={"gz": d},
-                device_id_type=MESH,
-            ).start()
-        pltpu.make_async_copy(part(mz), r2.at[mz, rows], ls2.at[i]).start()
-
-    @pl.loop(0, CH)
-    def _(i):
-        rows = pl.ds(CX * i, CX)
-        got = r2.at[pl.ds(0, GZ - 1), rows]
-        pltpu.make_async_copy(got, got, rs2.at[i]).wait()
-        own = r2.at[0, rows]
-        pltpu.make_async_copy(own, own, ls2.at[i]).wait()
+            bh[...] = high
+            bl[...] = low
+            for q in range(2):
+                table = 2 * chip + q
+                y1[q, x] = product(fyh[table], fyl[table], bh[...], bl[...])
+
+        away, stay = quarters(i)
+        away.start()
+        stay.start()
+        away.wait_recv()
+        stay.wait()
 
         @pl.loop(0, CX // 2)
         def _(k):
             x = CX * i + 2 * k
             for j in range(2):
-                line = jnp.concatenate([r2[d, x + j] for d in range(GZ)], axis=1)
+                line = jnp.concatenate([r2[0, x + j], r2[1, x + j]], axis=1)
                 high, low = split(line)
                 ah[j * YF : (j + 1) * YF] = high
                 al[j * YF : (j + 1) * YF] = low
@@ -320,44 +367,45 @@
                     ql[lines, 512 * n + 256 : 512 * n + 512] = low
             out = product(qh[...], ql[...], wih[...], wil[...])
             for j in range(2):
-                for d in range(GZ):
-                    zi[d, x + j] = out[j * YF : (j + 1) * YF, d * LANES : (d + 1) * LANES]
-
-        mine = r3.at[rows, pl.ds(pl.multiple_of(YF * mz, YF), YF), :]
-        for k in range(1, GZ):
-            d = lax.rem(mz + k, GZ)
-            pltpu.make_async_remote_copy(
-                src_ref=zi.at[d, rows],
-                dst_ref=mine,
-                send_sem=ss3.at[i],
-                recv_sem=rs3.at[i],
-                device_id={"gz": d},
-                device_id_type=MESH,
-            ).start()
-        pltpu.make_async_copy(zi.at[mz, rows], mine, ls3.at[i]).start()
-
-    @pl.loop(0, CH)
-    def _(i):
-        rows = pl.ds(CX * i, CX)
-        got = r3.at[rows, pl.ds(0, PAD - YF), :]
-        pltpu.make_async_copy(got, got, rs3.at[i]).wait()
-        own = r3.at[rows, pl.ds(0, YF), :]
-        pltpu.make_async_copy(own, own, ls3.at[i]).wait()
-
-        @pl.loop(0, CX // 2)
+                for d in range(2):
+                    zi[d, x + j] = out[j * YF : (j + 1) * YF, d * 256 : (d + 1) * 256]
+
+        away, stay = blocks(i)
+        away.start()
+        stay.start()
+        away.wait_recv()
+        stay.wait()
+
+        @pl.loop(0, CX)
         def _(k):
-            x = CX * i + 2 * k
-            pair = jnp.concatenate([r3[x], r3[x + 1]], axis=1)
-            full = jnp.concatenate([pair, turned_pair(pair, sign)], axis=0)
+            x = CX * i + k
+            both = r3[x]
+            full = jnp.concatenate([both, turned_pair(both, sign)], axis=0)
             high, low = split(full)
             bh[...] = high
             bl[...] = low
-            out = product(fyih[...], fyil[...], bh[...], bl[...])
-            yi[x] = out[:, :LANES]
-            yi[x + 1] = out[:, LANES:]
+            out = product(fyih[chip], fyil[chip], bh[...], bl[...])
+            for b in range(2):
+                yp[b, x] = out[:, b * LANES : (b + 1) * LANES].reshape(4, 2, 32, LANES)
+
+        for copy in partials(i):
+            copy.start()
+
+    @pl.loop(0, CH)
+    def _(i):
+        for copy in partials(i):
+            copy.wait_recv()
+
+        @pl.loop(0, CX)
+        def _(k):
+            x = CX * i + k
+            yi[0, x] = yp[chip, x, :, side] + yr[0, x]
+            yi[1, x] = yp[1 - chip, x, :, 1 - side] + yr[1, x]
 
         def part(p):
-            return yi.at[rows, pl.ds(pl.multiple_of(ROWS * p, ROWS), ROWS), :]
+            group, pair, first = place(p)
+            other = jnp.where(pair == side, 0, 1)
+            return yi.at[other, pl.ds(CX * i, CX), group, pl.ds(first, ROWS)]
 
         mine = r4.at[i, pl.ds(CX * me, CX)]
 
@@ -367,22 +415,19 @@
             pltpu.make_async_remote_copy(
                 src_ref=part(p),
                 dst_ref=mine,
-                send_sem=ss4.at[i],
-                recv_sem=rs4.at[i],
-                device_id={"gy": p},
+                send_sem=ss6.at[i],
+                recv_sem=rs6.at[i],
+                device_id=across(p),
                 device_id_type=MESH,
             ).start()
 
-        pltpu.make_async_copy(part(me), mine, ls4.at[i]).start()
+        pltpu.make_async_copy(part(me), mine, rs6.at[i]).start()
 
     acc[...] = jnp.zeros_like(acc)
 
     @pl.loop(0, CH)
     def _(i):
-        got = r4.at[i, pl.ds(0, CX * (GY - 1))]
-        pltpu.make_async_copy(got, got, rs4.at[i]).wait()
-        own = r4.at[i, pl.ds(0, CX)]
-        pltpu.make_async_copy(own, own, ls4.at[i]).wait()
+        pltpu.make_async_copy(r4.at[i], r4.at[i], rs6.at[i]).wait()
         lh, ll = fxih[i], fxil[i]
         for k in range(ROWS // 2):
             pair = jnp.concatenate([r4[i, :, 2 * k, :], r4[i, :, 2 * k + 1, :]], axis=1)
@@ -459,15 +504,13 @@
 
     @pl.loop(0, CH)
     def _(i):
-        rows = pl.ds(CX * i, CX)
         sent = s1.at[i, pl.ds(0, CX * (GY - 1))]
         pltpu.make_async_copy(sent, sent, ss1.at[i]).wait()
-        sent = r2.at[pl.ds(0, GZ - 1), rows]
-        pltpu.make_async_copy(sent, sent, ss2.at[i]).wait()
-        sent = zi.at[pl.ds(0, GZ - 1), rows]
-        pltpu.make_async_copy(sent, sent, ss3.at[i]).wait()
-        sent = yi.at[rows, pl.ds(0, NY - ROWS), :]
-        pltpu.make_async_copy(sent, sent, ss4.at[i]).wait()
+        for copy in gathered(i) + partials(i):
+            copy.wait_send()
+        quarters(i)[0].wait_send()
+        blocks(i)[0].wait_send()
+        pltpu.make_async_copy(sent, sent, ss6.at[i]).wait()
 
 
 def shards(source, contrast, green, forward_field, density, thresh_index):
@@ -491,16 +534,18 @@
         block((ROWS, 2 * NX, LANES), BF16),
         block((ROWS, 2 * NX, LANES), BF16),
         block((CH, GY * CX, ROWS, LANES), F32),
-        block((XF, NY, LANES), F32),
-        block((XF, PAD, LANES), F32),
-        block((GZ, XF, YF, LANES), F32),
-        block((GZ, XF, YF, LANES), F32),
-        block((XF, PAD, LANES), F32),
-        block((XF, NY, LANES), F32),
+        block((2, XF, 4, 2, 32, LANES), F32),
+        block((2, XF, YF, 2 * LANES), F32),
+        block((2, XF, YF, 2 * LANES), F32),
+        block((2, XF, YF, 2 * LANES), F32),
+        block((XF, 2 * YF, 2 * LANES), F32),
+        block((2, XF, 4, 2, 32, LANES), F32),
+        block((2, XF, 4, 32, LANES), F32),
+        block((2, XF, 4, 32, LANES), F32),
         block((CH, GY * CX, ROWS, LANES), F32),
         block((ROWS // 2, NX, 2 * LANES), F32),
-        block((2 * PAD, 2 * LANES), BF16),
-        block((2 * PAD, 2 * LANES), BF16),
+        block((PAD, 2 * LANES), BF16),
+        block((PAD, 2 * LANES), BF16),
         block((2 * YF, 2 * NZ), BF16),
         block((2 * YF, 2 * NZ), BF16),
         block((2 * YF, 2 * PAD), BF16),
@@ -512,9 +557,10 @@
         dma((4,)),
         dma((14,)),
     ]
-    scratch += [dma((CH,)) for _ in range(12)]
     scratch += [dma((2,)) for _ in range(4)]
     scratch += [dma((3, GZ)), dma((3, 2))]
+    scratch += [dma((CH,))] * 2 + [dma((CH, 2))] * 2
+    scratch += [dma((CH,))] * 6 + [dma((CH, 2))] * 2 + [dma((CH,))] * 2
     return pl.pallas_call(
         kernel,
         out_shape=(

time: 168 us -> 143 us (0.85)
  Pallas kernels: 161 us -> 135 us
    pallas_call x1, Pallas kernels: 161 us -> 135 us  [shards(): pl.pallas_call(kernel, out_shape=(jax.ShapeDtypeStruct((2, ROWS, DEPTH, N...]
where the time goes in v2:
time: 143 us; the launch traced here: 142 us
  Pallas kernels  135 us (94%)
  local copies, waits for them, and re-layouts  5.65 us (4%)
    pallas_call x1, Pallas kernels, shards(): pl.pallas_call(kernel, out_shape=(jax.ShapeDtypeStruct((2, ROWS, DEPTH, N...  135 us
    unnamed x3, local copies, waits for them, and re-layouts  4.88 us

profile of v2, /device:TPU:1, one launch (start us, length us, event | category | flops | bytes accessed | tf_op | source)
XLA Modules:
  0.0 142.2 jit_solution(10245499686969783000)
XLA Ops:
  0.6 0.7 multiply_add_fusion
  1.3 0.1 broadcast_in_dim.2
  1.4 0.7 reshape.10.refs_5_
  2.1 135.3 %shard_map.211 = (f32[2,8,64,256]{3,2,1,0:T(8,128)}, f32[8,256]{1,0:T(8,128)}, f32[8,256]{1,0:T(8,128)}) custom-call(f32[2,8,64,256]{3,2,1,0:T(8,128)} %refs_0_.1, f32[8,64,256]{2,1,0:T(8,128)} %refs_1_.1, f32[2,8,64,256]{3,2,1,0:T(8,128)} %refs_2_.1, f32[2,16,128,512]{3,2,1,0:T(8,128)} %refs_3_.1, f32[8,256]{1,0:T(8,128)} %refs_4_.1, ...), custom_call_target="tpu_custom_call" | custom-call | tf_op jit(solution)/shard_map/pallas_call | solution.py:564
  137.3 2.3 %copy.26 = f32[2,8,64,256]{3,2,1,0:T(8,128)} copy(f32[2,8,64,256]{3,2,1,0:T(8,128)} %get-tuple-element.6) | data formatting | bytes 2097152
  139.6 1.3 copy.27
  140.9 1.3 copy.28

commit v3 on v2

--- a/solution.py
+++ b/solution.py
@@ -26,8 +26,10 @@
 XF = PAD // GY
 YF = PAD // GZ
 LANES = 2 * DEPTH
-CH = 4
+CH = 8
 CX = XF // CH
+LAST = 6
+JOIN = CH // 4
 
 F32 = jnp.float32
 BF16 = jnp.bfloat16
@@ -47,6 +49,7 @@
     cos, sin = np.cos(angle), np.sin(angle)
     order = np.arange(PAD).reshape(GY, CH, CX).transpose(1, 0, 2).reshape(CH, GY * CX)
     fx = np.concatenate([cos[order], sin[order]], axis=2)
+    joined = order.reshape(CH // JOIN, JOIN * GY * CX)
     fy = np.concatenate([cos, sin], axis=1).reshape(GZ, YF, 2 * NY)
     half = (2, PAD // 2, NY)
     fyi = np.concatenate(
@@ -54,7 +57,7 @@
         axis=2,
     )
     fxi = np.concatenate(
-        [cos[order].transpose(0, 2, 1), -sin[order].transpose(0, 2, 1)], axis=2
+        [cos[joined].transpose(0, 2, 1), -sin[joined].transpose(0, 2, 1)], axis=2
     )
     shape = (2, 256, 2, 2, DEPTH)
     ct = cos.reshape(shape).transpose(0, 3, 2, 4, 1)
@@ -131,14 +134,8 @@
     fills = [
         pltpu.make_async_copy(tabs_h[n], tabs[n], tab_sem.at[n]) for n in range(14)
     ]
-    loads[0].start()
-    loads[1].start()
-    for n in range(12):
-        fills[n].start()
-    loads[3].start()
-    fills[12].start()
-    fills[13].start()
-    loads[2].start()
+    for copy in (loads[0], loads[1], fills[0], fills[1]):
+        copy.start()
 
     barrier = pltpu.get_barrier_semaphore()
 
@@ -163,6 +160,8 @@
 
     loads[0].wait()
     loads[1].wait()
+    for copy in fills[12:] + fills[2:6] + fills[8:12] + loads[3:] + fills[6:8] + loads[2:3]:
+        copy.start()
 
     @pl.loop(0, ROWS)
     def _(y):
@@ -194,8 +193,7 @@
     for copy in near_copies:
         copy.start()
 
-    @pl.loop(0, CH)
-    def _(i):
+    def forward_x(i):
         lh, ll = fxh[i], fxl[i]
         for k in range(ROWS // 2):
             rh = jnp.concatenate([sth[2 * k], sth[2 * k + 1]], axis=1)
@@ -224,11 +222,6 @@
 
         pltpu.make_async_copy(part(me), mine, rs1.at[i]).start()
 
-    fills[12].wait()
-    fills[13].wait()
-    for copy in near_copies:
-        copy.wait()
-
     def wide(buffer):
         rows = jnp.concatenate(
             [buffer[0][ROWS - RADIUS :], buffer[2], buffer[1][:RADIUS]], axis=0
@@ -252,17 +245,23 @@
     exact = functools.partial(
         jnp.dot, preferred_element_type=F32, precision=lax.Precision.HIGHEST
     )
-    smooth = tent_rows(wide(near)) / weight16[RADIUS : RADIUS + ROWS]
-    filtered = exact(smooth, filt_t[...])
-    threshold = level[...]
-    steep = jnp.tanh(SHARP * (filtered - threshold))
-    shift = jnp.tanh(SHARP * threshold)
-    below = shift + jnp.tanh(SHARP * (1.0 - threshold))
-    proj[...] = (shift + steep) / below
-    fact[2] = SHARP * (1.0 - steep * steep) / below
     fact_copies = [near_copy(fact, 0, after, sf, rf), near_copy(fact, 1, before, sf, rf)]
-    for copy in fact_copies:
-        copy.start()
+
+    def project():
+        fills[12].wait()
+        fills[13].wait()
+        for copy in near_copies:
+            copy.wait()
+        smooth = tent_rows(wide(near)) / weight16[RADIUS : RADIUS + ROWS]
+        filtered = exact(smooth, filt_t[...])
+        threshold = level[...]
+        steep = jnp.tanh(SHARP * (filtered - threshold))
+        shift = jnp.tanh(SHARP * threshold)
+        below = shift + jnp.tanh(SHARP * (1.0 - threshold))
+        proj[...] = (shift + steep) / below
+        fact[2] = SHARP * (1.0 - steep * steep) / below
+        for copy in fact_copies:
+            copy.start()
 
     def swap(source, target, i, sends, recvs):
         return [
@@ -308,19 +307,13 @@
         pieces = [yp.at[1 - chip, rows, :, side], yp.at[chip, rows, :, 1 - side]]
         return swap(pieces, [yr.at[n, rows] for n in range(2)], i, ss5, rs5)
 
-    @pl.loop(0, CH)
-    def _(i):
+    def gather(i):
         whole = r1.at[0, pl.ds(CX * i, CX)]
         pltpu.make_async_copy(whole, whole, rs1.at[i]).wait()
         for copy in gathered(i):
             copy.start()
 
-    for n in range(2, 12):
-        fills[n].wait()
-    loads[3].wait()
-
-    @pl.loop(0, CH)
-    def _(i):
+    def forward_y(i):
         for copy in gathered(i):
             copy.wait_recv()
 
@@ -341,6 +334,9 @@
         away, stay = quarters(i)
         away.start()
         stay.start()
+
+    def along_z(i):
+        away, stay = quarters(i)
         away.wait_recv()
         stay.wait()
 
@@ -373,6 +369,9 @@
         away, stay = blocks(i)
         away.start()
         stay.start()
+
+    def inverse_y(i):
+        away, stay = blocks(i)
         away.wait_recv()
         stay.wait()
 
@@ -391,8 +390,7 @@
         for copy in partials(i):
             copy.start()
 
-    @pl.loop(0, CH)
-    def _(i):
+    def add_halves(i):
         for copy in partials(i):
             copy.wait_recv()
 
@@ -423,17 +421,56 @@
 
         pltpu.make_async_copy(part(me), mine, rs6.at[i]).start()
 
-    acc[...] = jnp.zeros_like(acc)
-
-    @pl.loop(0, CH)
-    def _(i):
-        pltpu.make_async_copy(r4.at[i], r4.at[i], rs6.at[i]).wait()
-        lh, ll = fxih[i], fxil[i]
+    def inverse_x(last):
+        j = last // JOIN
+        for n in range(JOIN):
+            whole = r4.at[JOIN * j + n]
+            pltpu.make_async_copy(whole, whole, rs6.at[JOIN * j + n]).wait()
+        lh, ll = fxih[j], fxil[j]
+
+        def lines(y):
+            return jnp.concatenate([r4[JOIN * j + n, :, y, :] for n in range(JOIN)], axis=0)
+
         for k in range(ROWS // 2):
-            pair = jnp.concatenate([r4[i, :, 2 * k, :], r4[i, :, 2 * k + 1, :]], axis=1)
+            pair = jnp.concatenate([lines(2 * k), lines(2 * k + 1)], axis=1)
             full = jnp.concatenate([pair, turned_pair(pair, sign)], axis=0)
             high, low = split(full)
             acc[k] += product(lh, ll, high, low)
+
+    def join_x(i):
+        @pl.when(lax.rem(i, JOIN) == JOIN - 1)
+        def _():
+            inverse_x(i)
+
+    acc[...] = jnp.zeros_like(acc)
+
+    @pl.loop(0, CH + LAST)
+    def _(step):
+        def stage(lag, work):
+            i = step - lag
+
+            @pl.when((i >= 0) & (i < CH))
+            def _():
+                work(i)
+
+        stage(0, forward_x)
+
+        @pl.when(step == 1)
+        def _():
+            for n in range(2, 12):
+                fills[n].wait()
+            loads[3].wait()
+
+        stage(1, gather)
+        stage(4, inverse_y)
+        stage(3, along_z)
+        stage(5, add_halves)
+        stage(2, forward_y)
+        stage(LAST, join_x)
+
+        @pl.when(step == 2)
+        def _():
+            project()
 
     scale = 1.0 / float(PAD) ** 3
 

time: 143 us -> 134 us (0.937)
  Pallas kernels: 135 us -> 127 us
    pallas_call x1, Pallas kernels: 135 us -> 127 us  [shards(): pl.pallas_call(kernel, out_shape=(jax.ShapeDtypeStruct((2, ROWS, DEPTH, N...]
where the time goes in v3:
time: 134 us
  Pallas kernels  127 us (95%)
  local copies, waits for them, and re-layouts  5.65 us (4%)
    pallas_call x1, Pallas kernels, shards(): pl.pallas_call(kernel, out_shape=(jax.ShapeDtypeStruct((2, ROWS, DEPTH, N...  127 us
    unnamed x3, local copies, waits for them, and re-layouts  4.88 us

profile of v3, /device:TPU:1, one launch (start us, length us, event | category | flops | bytes accessed | tf_op | source)
XLA Modules:
  0.0 134.0 jit_solution(5359284365886735189)
XLA Ops:
  0.6 0.7 multiply_add_fusion
  1.3 0.1 broadcast_in_dim.2
  1.4 0.7 reshape.10.refs_5_
  2.1 127.0 %shard_map.211 = (f32[2,8,64,256]{3,2,1,0:T(8,128)}, f32[8,256]{1,0:T(8,128)}, f32[8,256]{1,0:T(8,128)}) custom-call(f32[2,8,64,256]{3,2,1,0:T(8,128)} %refs_0_.1, f32[8,64,256]{2,1,0:T(8,128)} %refs_1_.1, f32[2,8,64,256]{3,2,1,0:T(8,128)} %refs_2_.1, f32[2,16,128,512]{3,2,1,0:T(8,128)} %refs_3_.1, f32[8,256]{1,0:T(8,128)} %refs_4_.1, ...), custom_call_target="tpu_custom_call" | custom-call | tf_op jit(solution)/shard_map/pallas_call | solution.py:601
  129.1 2.3 %copy.26 = f32[2,8,64,256]{3,2,1,0:T(8,128)} copy(f32[2,8,64,256]{3,2,1,0:T(8,128)} %get-tuple-element.6) | data formatting | bytes 2097152
  131.4 1.3 copy.27
  132.7 1.3 copy.28

commit v4 on v3

--- a/solution.py
+++ b/solution.py
@@ -28,6 +28,9 @@
 LANES = 2 * DEPTH
 CH = 8
 CX = XF // CH
+EXTRA = 4
+BOTH = ROWS + EXTRA
+EARLY = 2
 LAST = 6
 JOIN = CH // 4
 
@@ -50,7 +53,9 @@
     order = np.arange(PAD).reshape(GY, CH, CX).transpose(1, 0, 2).reshape(CH, GY * CX)
     fx = np.concatenate([cos[order], sin[order]], axis=2)
     joined = order.reshape(CH // JOIN, JOIN * GY * CX)
-    fy = np.concatenate([cos, sin], axis=1).reshape(GZ, YF, 2 * NY)
+    by_pair = np.arange(NY).reshape(4, 2, 32).transpose(1, 0, 2).reshape(NY)
+    fy = np.concatenate([cos[:, by_pair], sin[:, by_pair]], axis=1)
+    fy = fy.reshape(GZ, YF, 2 * NY)
     half = (2, PAD // 2, NY)
     fyi = np.concatenate(
         [cos.reshape(half).transpose(0, 2, 1), -sin.reshape(half).transpose(0, 2, 1)],
@@ -65,7 +70,7 @@
     re_rows = np.concatenate([ct, -st], axis=4)
     im_rows = np.concatenate([st, ct], axis=4)
     wz = np.stack([re_rows, im_rows], axis=3).reshape(2, 2 * NZ, 512)
-    wzi = wz.transpose(0, 2, 1).reshape(1024, 512)
+    wzi = wz.transpose(0, 2, 1).reshape(1024, 2, 256).transpose(1, 0, 2)
     flat = []
     for table in (fx, fy, fyi, fxi, wz, wzi):
         flat.extend(halves(table))
@@ -104,9 +109,10 @@
     (src, con, fwd, green) = refs[23:27]
     tabs = refs[27:41]
     (sth, stl, s1, r1, y1, r2, zi, r3, yp, yr, yi, r4, acc) = refs[41:54]
+    (raw, sw, rw) = refs[86:89]
     (bh, bl, ah, al, qh, ql, near, fact, slab, slabs) = refs[54:64]
     (in_sem, tab_sem, sn, rn, sf, rf, sp, rp) = refs[64:72]
-    (ss1, rs1, ss2, rs2, ss3, rs3, ls3, ss4, rs4, ls4, ss5, rs5, ss6, rs6) = refs[72:86]
+    (ss1, rs1, ss2, rs2, ss3, rs3, _, ss4, rs4, _, ss5, rs5, ss6, rs6) = refs[72:86]
     fxh, fxl, fyh, fyl, fyih, fyil, fxih, fxil, wzh, wzl, wih, wil, filt, filt_t = tabs
 
     me = lax.axis_index("gy")
@@ -118,7 +124,7 @@
     partner = lax.rem(mz + 2, GZ)
 
     def place(p):
-        return p // 8, lax.rem(p // 4, 2), pl.multiple_of(ROWS * lax.rem(p, 4), ROWS)
+        return p // 8, lax.rem(p // 4, 2), lax.rem(p, 4)
 
     def across(p):
         same = lax.rem(p // 4, 2) == side
@@ -163,20 +169,43 @@
     for copy in fills[12:] + fills[2:6] + fills[8:12] + loads[3:] + fills[6:8] + loads[2:3]:
         copy.start()
 
-    @pl.loop(0, ROWS)
-    def _(y):
+    def stimulus(y):
         weight = con[y]
         both = jnp.concatenate([src[0, y] * weight, src[1, y] * weight], axis=0)
-        flat = both.T
+        return both.T
+
+    def keep(y, flat):
         full = jnp.concatenate([flat, turned(flat, sign)], axis=0)
         high, low = split(full)
         sth[y] = high
         stl[y] = low
 
+    @pl.loop(0, EXTRA)
+    def _(y):
+        raw[0, y] = stimulus(y)
+
+    pl.semaphore_wait(barrier, (GY - 1) + 2 * GZ + (GZ - 1))
+
+    shared = pltpu.make_async_remote_copy(
+        src_ref=raw.at[0],
+        dst_ref=raw.at[1],
+        send_sem=sw,
+        recv_sem=rw,
+        device_id={"gz": partner},
+        device_id_type=MESH,
+    )
+    shared.start()
+
+    @pl.loop(0, EXTRA)
+    def _(y):
+        keep(y, raw[0, y])
+
+    @pl.loop(EXTRA, ROWS)
+    def _(y):
+        keep(y, stimulus(y))
+
     fills[0].wait()
     fills[1].wait()
-
-    pl.semaphore_wait(barrier, (GY - 1) + 2 * GZ + (GZ - 1))
 
     def near_copy(buffer, slot, target, sems, recv):
         return pltpu.make_async_remote_copy(
@@ -193,20 +222,48 @@
     for copy in near_copies:
         copy.start()
 
+    def take_shared():
+        shared.wait()
+
+        @pl.loop(0, EXTRA)
+        def _(y):
+            keep(ROWS + y, raw[1, y])
+
+    def by_extra(i, work):
+        @pl.when(i < EARLY)
+        def _():
+            work(i, 0)
+
+        @pl.when(i >= EARLY)
+        def _():
+            work(i, EXTRA)
+
     def forward_x(i):
-        lh, ll = fxh[i], fxl[i]
-        for k in range(ROWS // 2):
+        def rows(k):
             rh = jnp.concatenate([sth[2 * k], sth[2 * k + 1]], axis=1)
             rl = jnp.concatenate([stl[2 * k], stl[2 * k + 1]], axis=1)
-            out = product(lh, ll, rh, rl)
+            out = product(fxh[i], fxl[i], rh, rl)
             s1[i, :, 2 * k, :] = out[:, :LANES]
             s1[i, :, 2 * k + 1, :] = out[:, LANES:]
 
+        for k in range(ROWS // 2):
+            rows(k)
+
+        @pl.when(i >= EARLY)
+        def _():
+            for k in range(ROWS // 2, BOTH // 2):
+                rows(k)
+
+        by_extra(i, spread_x)
+
+    def spread_x(i, extra):
+        count = pl.ds(0, ROWS + extra)
+
         def part(p):
-            return s1.at[i, pl.ds(CX * p, CX)]
-
-        group, pair, first = place(me)
-        mine = r1.at[chip, pl.ds(CX * i, CX), group, pair, pl.ds(first, ROWS)]
+            return s1.at[i, pl.ds(CX * p, CX), count]
+
+        group, pair, rank = place(me)
+        mine = r1.at[pl.ds(CX * i, CX), group, pair, rank, count]
 
         @pl.loop(1, GY)
         def _(k):
@@ -254,7 +311,13 @@
             copy.wait()
         smooth = tent_rows(wide(near)) / weight16[RADIUS : RADIUS + ROWS]
         filtered = exact(smooth, filt_t[...])
-        threshold = level[...]
+        levels = 0.35 + 0.1 * level[...].astype(F32)
+        tile = lax.broadcasted_iota(jnp.int32, (2, NX), 1) // TILE_X
+        wide_levels = jnp.zeros((2, NX), F32)
+        for n in range(NX // TILE_X):
+            wide_levels = jnp.where(tile == n, levels[:, n : n + 1], wide_levels)
+        upper = lax.broadcasted_iota(jnp.int32, (ROWS, NX), 0) < TILE_Y
+        threshold = jnp.where(upper, wide_levels[0:1], wide_levels[1:2])
         steep = jnp.tanh(SHARP * (filtered - threshold))
         shift = jnp.tanh(SHARP * threshold)
         below = shift + jnp.tanh(SHARP * (1.0 - threshold))
@@ -263,23 +326,16 @@
         for copy in fact_copies:
             copy.start()
 
-    def swap(source, target, i, sends, recvs):
-        return [
-            pltpu.make_async_remote_copy(
-                src_ref=source[n],
-                dst_ref=target[n],
-                send_sem=sends.at[i, n],
-                recv_sem=recvs.at[i, n],
-                device_id={"gz": partner},
-                device_id_type=MESH,
-            )
-            for n in range(2)
-        ]
-
-    def gathered(i):
-        rows = pl.ds(CX * i, CX)
-        pieces = [r1.at[chip, rows, :, side], r1.at[1 - chip, rows, :, 1 - side]]
-        return swap(pieces, pieces, i, ss2, rs2)
+    def gathered(i, extra):
+        lines = r1.at[pl.ds(CX * i, CX)]
+        return pltpu.make_async_remote_copy(
+            src_ref=lines.at[:, :, :, :, pl.ds(extra, ROWS - extra)],
+            dst_ref=lines.at[:, :, :, :, pl.ds(ROWS + extra, ROWS - extra)],
+            send_sem=ss2.at[i],
+            recv_sem=rs2.at[i],
+            device_id={"gz": partner},
+            device_id_type=MESH,
+        )
 
     def to_sibling(source, target, i, send, recv):
         return pltpu.make_async_remote_copy(
@@ -293,52 +349,65 @@
 
     def quarters(i):
         rows = pl.ds(CX * i, CX)
-        away = to_sibling(y1.at[1 - core, rows], r2.at[core, rows], i, ss3, rs3)
-        return away, pltpu.make_async_copy(y1.at[core, rows], r2.at[core, rows], ls3.at[i])
+        return to_sibling(y1.at[rows], r2.at[core, rows], i, ss3, rs3)
 
     def blocks(i):
         rows = pl.ds(CX * i, CX)
         mine = r3.at[rows, pl.ds(pl.multiple_of(YF * core, YF), YF), :]
-        away = to_sibling(zi.at[1 - core, rows], mine, i, ss4, rs4)
-        return away, pltpu.make_async_copy(zi.at[core, rows], mine, ls4.at[i])
+        return to_sibling(zi.at[rows], mine, i, ss4, rs4)
 
     def partials(i):
         rows = pl.ds(CX * i, CX)
         pieces = [yp.at[1 - chip, rows, :, side], yp.at[chip, rows, :, 1 - side]]
-        return swap(pieces, [yr.at[n, rows] for n in range(2)], i, ss5, rs5)
+        return [
+            pltpu.make_async_remote_copy(
+                src_ref=pieces[n],
+                dst_ref=yr.at[n, rows],
+                send_sem=ss5.at[i, n],
+                recv_sem=rs5.at[i, n],
+                device_id={"gz": partner},
+                device_id_type=MESH,
+            )
+            for n in range(2)
+        ]
 
     def gather(i):
-        whole = r1.at[0, pl.ds(CX * i, CX)]
-        pltpu.make_async_copy(whole, whole, rs1.at[i]).wait()
-        for copy in gathered(i):
-            copy.start()
+        def pass_on(i, extra):
+            whole = r1.at[pl.ds(CX * i, CX), :, :, :, pl.ds(0, ROWS + extra)]
+            pltpu.make_async_copy(whole, whole, rs1.at[i]).wait()
+            gathered(i, extra).start()
+
+        by_extra(i, pass_on)
 
     def forward_y(i):
-        for copy in gathered(i):
-            copy.wait_recv()
+        by_extra(i, lambda i, extra: gathered(i, extra).wait_recv())
 
         @pl.loop(0, CX)
         def _(k):
             x = CX * i + k
-            both = jnp.concatenate(
-                [r1[0, x].reshape(NY, LANES), r1[1, x].reshape(NY, LANES)], axis=1
-            )
+
+            def block_of(b):
+                parts = []
+                for pair in range(2):
+                    first = jnp.where(pair == side, chip, 1 - chip)
+                    at = pl.multiple_of(jnp.where(first == b, 0, ROWS), ROWS)
+                    lines = r1[x, :, pair, :, pl.ds(at, ROWS), :]
+                    parts.append(lines.reshape(NY // 2, LANES))
+                return jnp.concatenate(parts, axis=0)
+
+            both = jnp.concatenate([block_of(0), block_of(1)], axis=1)
             full = jnp.concatenate([both, turned_pair(both, sign)], axis=0)
             high, low = split(full)
             bh[...] = high
             bl[...] = low
-            for q in range(2):
-                table = 2 * chip + q
-                y1[q, x] = product(fyh[table], fyl[table], bh[...], bl[...])
-
-        away, stay = quarters(i)
-        away.start()
-        stay.start()
+            here, there = 2 * chip + core, 2 * chip + 1 - core
+            y1[x] = product(fyh[there], fyl[there], bh[...], bl[...])
+            r2[core, x] = product(fyh[here], fyl[here], bh[...], bl[...])
+
+        quarters(i).start()
 
     def along_z(i):
-        away, stay = quarters(i)
-        away.wait_recv()
-        stay.wait()
+        quarters(i).wait_recv()
 
         @pl.loop(0, CX // 2)
         def _(k):
@@ -361,19 +430,19 @@
                     high, low = split(real * g_imag + imag * g_real)
                     qh[lines, 512 * n + 256 : 512 * n + 512] = high
                     ql[lines, 512 * n + 256 : 512 * n + 512] = low
-            out = product(qh[...], ql[...], wih[...], wil[...])
+            out = product(qh[...], ql[...], wih[1 - core], wil[1 - core])
             for j in range(2):
-                for d in range(2):
-                    zi[d, x + j] = out[j * YF : (j + 1) * YF, d * 256 : (d + 1) * 256]
-
-        away, stay = blocks(i)
-        away.start()
-        stay.start()
+                zi[x + j] = out[j * YF : (j + 1) * YF]
+            out = product(qh[...], ql[...], wih[core], wil[core])
+            for j in range(2):
+                r3[x + j, pl.ds(pl.multiple_of(YF * core, YF), YF), :] = out[
+                    j * YF : (j + 1) * YF
+                ]
+
+        blocks(i).start()
 
     def inverse_y(i):
-        away, stay = blocks(i)
-        away.wait_recv()
-        stay.wait()
+        blocks(i).wait_recv()
 
         @pl.loop(0, CX)
         def _(k):
@@ -401,8 +470,9 @@
             yi[1, x] = yp[1 - chip, x, :, 1 - side] + yr[1, x]
 
         def part(p):
-            group, pair, first = place(p)
+            group, pair, rank = place(p)
             other = jnp.where(pair == side, 0, 1)
+            first = pl.multiple_of(ROWS * rank, ROWS)
             return yi.at[other, pl.ds(CX * i, CX), group, pl.ds(first, ROWS)]
 
         mine = r4.at[i, pl.ds(CX * me, CX)]
@@ -452,6 +522,10 @@
             @pl.when((i >= 0) & (i < CH))
             def _():
                 work(i)
+
+        @pl.when(step == EARLY)
+        def _():
+            take_shared()
 
         stage(0, forward_x)
 
@@ -541,20 +615,25 @@
 
     @pl.loop(0, CH)
     def _(i):
-        sent = s1.at[i, pl.ds(0, CX * (GY - 1))]
-        pltpu.make_async_copy(sent, sent, ss1.at[i]).wait()
-        for copy in gathered(i) + partials(i):
+        def leave(i, extra):
+            sent = s1.at[i, pl.ds(0, CX * (GY - 1)), pl.ds(0, ROWS + extra)]
+            pltpu.make_async_copy(sent, sent, ss1.at[i]).wait()
+            gathered(i, extra).wait_send()
+
+        by_extra(i, leave)
+        for copy in [quarters(i), blocks(i)] + partials(i):
             copy.wait_send()
-        quarters(i)[0].wait_send()
-        blocks(i)[0].wait_send()
+        sent = r4.at[i, pl.ds(0, CX * (GY - 1))]
         pltpu.make_async_copy(sent, sent, ss6.at[i]).wait()
 
 
+def hand_over(adj, proj, grad, adj_out, proj_out, grad_out):
+    adj_out[...] = adj[...]
+    proj_out[...] = proj[...]
+    grad_out[...] = grad[...]
+
+
 def shards(source, contrast, green, forward_field, density, thresh_index):
-    levels = 0.35 + 0.1 * thresh_index.astype(F32)
-    threshold = jnp.broadcast_to(
-        levels[:, None, :, None], (levels.shape[0], TILE_Y, levels.shape[1], TILE_X)
-    ).reshape(ROWS, NX)
     constants = tables()
     anywhere = pl.BlockSpec(memory_space=pl.ANY)
     vmem = pl.BlockSpec(memory_space=pltpu.VMEM)
@@ -568,13 +647,13 @@
     ]
     scratch += [block(table.shape, table.dtype) for table in constants]
     scratch += [
-        block((ROWS, 2 * NX, LANES), BF16),
-        block((ROWS, 2 * NX, LANES), BF16),
-        block((CH, GY * CX, ROWS, LANES), F32),
-        block((2, XF, 4, 2, 32, LANES), F32),
+        block((BOTH, 2 * NX, LANES), BF16),
+        block((BOTH, 2 * NX, LANES), BF16),
+        block((CH, GY * CX, 2 * ROWS, LANES), F32),
+        block((XF, 4, 2, 4, 2 * ROWS, LANES), F32),
+        block((XF, YF, 2 * LANES), F32),
         block((2, XF, YF, 2 * LANES), F32),
-        block((2, XF, YF, 2 * LANES), F32),
-        block((2, XF, YF, 2 * LANES), F32),
+        block((XF, YF, 2 * LANES), F32),
         block((XF, 2 * YF, 2 * LANES), F32),
         block((2, XF, 4, 2, 32, LANES), F32),
         block((2, XF, 4, 32, LANES), F32),
@@ -596,9 +675,10 @@
     ]
     scratch += [dma((2,)) for _ in range(4)]
     scratch += [dma((3, GZ)), dma((3, 2))]
-    scratch += [dma((CH,))] * 2 + [dma((CH, 2))] * 2
+    scratch += [dma((CH,))] * 4
     scratch += [dma((CH,))] * 6 + [dma((CH, 2))] * 2 + [dma((CH,))] * 2
-    return pl.pallas_call(
+    scratch += [block((2, EXTRA, NX, LANES), F32), dma, dma]
+    results = pl.pallas_call(
         kernel,
         out_shape=(
             jax.ShapeDtypeStruct((2, ROWS, DEPTH, NX), F32),
@@ -611,7 +691,16 @@
         compiler_params=pltpu.CompilerParams(
             collective_id=0, has_side_effects=True, vmem_limit_bytes=62 << 20
         ),
-    )(source, contrast, forward_field, green, density, threshold, *map(jnp.asarray, constants))
+    )(source, contrast, forward_field, green, density, thresh_index, *map(jnp.asarray, constants))
+    pieces = [pl.BlockSpec((2, ROWS // 4, DEPTH, NX), lambda n: (0, n, 0, 0))]
+    pieces += [pl.BlockSpec((ROWS, NX), lambda n: (0, 0))] * 2
+    return pl.pallas_call(
+        hand_over,
+        out_shape=tuple(jax.ShapeDtypeStruct(r.shape, r.dtype) for r in results),
+        grid=(4,),
+        in_specs=pieces,
+        out_specs=tuple(pieces),
+    )(*results)
 
 
 def solution(mesh):

time: 134 us -> 121 us (0.903)
  Pallas kernels: 127 us -> 120 us
  local copies, waits for them, and re-layouts: 5.65 us -> 0 us
    pallas_call x1, Pallas kernels: 127 us -> 117 us  [shards(): pl.pallas_call(kernel, out_shape=(jax.ShapeDtypeStruct((2, ROWS, DEPTH, N...]
    unnamed x3 -> x0, local copies, waits for them, and re-layouts: 4.88 us -> none
    pallas_call x0 -> x1, Pallas kernels: none -> 3.39 us  [shards(): pl.pallas_call(hand_over, out_shape=tuple((jax.ShapeDtypeStruct(r.shape,...]
where the time goes in v4:
time: 121 us
  Pallas kernels  120 us (99%)
    pallas_call x1, Pallas kernels, shards(): pl.pallas_call(kernel, out_shape=(jax.ShapeDtypeStruct((2, ROWS, DEPTH, N...  117 us
    pallas_call x1, Pallas kernels, shards(): pl.pallas_call(hand_over, out_shape=tuple((jax.ShapeDtypeStruct(r.shape,...  3.39 us

profile of v4, /device:TPU:1, one launch (start us, length us, event | category | flops | bytes accessed | tf_op | source)
XLA Modules:
  0.0 120.8 jit_solution(4582539237431112059)
XLA Ops:
  0.6 116.7 %shard_map.211 = (f32[2,8,64,256]{3,2,1,0:T(8,128)}, f32[8,256]{1,0:T(8,128)}, f32[8,256]{1,0:T(8,128)}) custom-call(f32[2,8,64,256]{3,2,1,0:T(8,128)} %refs_0_.1, f32[8,64,256]{2,1,0:T(8,128)} %refs_1_.1, f32[2,8,64,256]{3,2,1,0:T(8,128)} %refs_2_.1, f32[2,16,128,512]{3,2,1,0:T(8,128)} %refs_3_.1, f32[8,256]{1,0:T(8,128)} %refs_4_.1, s32[2,16]{1,0:T(2,128)} %refs_5_.1, ...), custom_call_target="tpu_custom_call" | custom-call | tf_op jit(solution)/shard_map/pallas_call | solution.py:681
  117.4 3.4 %shard_map.212 = (f32[2,8,64,256]{3,2,1,0:T(8,128)}, f32[8,256]{1,0:T(8,128)}, f32[8,256]{1,0:T(8,128)}) custom-call(f32[2,8,64,256]{3,2,1,0:T(8,128)} %get-tuple-element.6.adj, f32[8,256]{1,0:T(8,128)} %get-tuple-element.7.proj, f32[8,256]{1,0:T(8,128)} %get-tuple-element.8.grad), custom_call_target="tpu_custom_call" | custom-call | tf_op jit(solution)/shard_map/pallas_call | solution.py:697

commit v5 on v4

--- a/solution.py
+++ b/solution.py
@@ -31,7 +31,7 @@
 EXTRA = 4
 BOTH = ROWS + EXTRA
 EARLY = 2
-LAST = 6
+LAST = 7
 JOIN = CH // 4
 
 F32 = jnp.float32
@@ -105,11 +105,11 @@
 def kernel(*refs):
     (src_h, con_h, fwd_h, green_h, dens, level) = refs[:6]
     tabs_h = refs[6:20]
-    adj, proj, grad = refs[20:23]
+    adj_h, proj, grad = refs[20:23]
     (src, con, fwd, green) = refs[23:27]
     tabs = refs[27:41]
     (sth, stl, s1, r1, y1, r2, zi, r3, yp, yr, yi, r4, acc) = refs[41:54]
-    (raw, sw, rw) = refs[86:89]
+    (raw, sw, rw, adj, out_sem) = refs[86:91]
     (bh, bl, ah, al, qh, ql, near, fact, slab, slabs) = refs[54:64]
     (in_sem, tab_sem, sn, rn, sf, rf, sp, rp) = refs[64:72]
     (ss1, rs1, ss2, rs2, ss3, rs3, _, ss4, rs4, _, ss5, rs5, ss6, rs6) = refs[72:86]
@@ -538,7 +538,7 @@
         stage(1, gather)
         stage(4, inverse_y)
         stage(3, along_z)
-        stage(5, add_halves)
+        stage(6, add_halves)
         stage(2, forward_y)
         stage(LAST, join_x)
 
@@ -554,6 +554,9 @@
             flat = acc[k, :, j * LANES : (j + 1) * LANES].T * scale
             adj[0, 2 * k + j] = src[0, 2 * k + j] - flat[:DEPTH]
             adj[1, 2 * k + j] = src[1, 2 * k + j] - flat[DEPTH:]
+
+    done = pltpu.make_async_copy(adj, adj_h, out_sem)
+    done.start()
 
     loads[2].wait()
     holds = (mz == 1) | (mz == 2)
@@ -612,6 +615,8 @@
     def _():
         for step, turn in reaches:
             slab_copy(step, turn).wait_send()
+
+    done.wait()
 
     @pl.loop(0, CH)
     def _(i):
@@ -678,6 +683,7 @@
     scratch += [dma((CH,))] * 4
     scratch += [dma((CH,))] * 6 + [dma((CH, 2))] * 2 + [dma((CH,))] * 2
     scratch += [block((2, EXTRA, NX, LANES), F32), dma, dma]
+    scratch += [block((2, ROWS, DEPTH, NX), F32), dma]
     results = pl.pallas_call(
         kernel,
         out_shape=(
@@ -686,7 +692,7 @@
             jax.ShapeDtypeStruct((ROWS, NX), F32),
         ),
         in_specs=[anywhere] * 4 + [vmem] * 2 + [anywhere] * 14,
-        out_specs=(vmem, vmem, vmem),
+        out_specs=(anywhere, vmem, vmem),
         scratch_shapes=scratch,
         compiler_params=pltpu.CompilerParams(
             collective_id=0, has_side_effects=True, vmem_limit_bytes=62 << 20

time: 121 us -> 120 us (level)
  no operation moved by 1% of the time
where the time goes in v5:
time: 120 us
  Pallas kernels  119 us (99%)
    pallas_call x1, Pallas kernels, shards(): pl.pallas_call(kernel, out_shape=(jax.ShapeDtypeStruct((2, ROWS, DEPTH, N...  116 us
    pallas_call x1, Pallas kernels, shards(): pl.pallas_call(hand_over, out_shape=tuple((jax.ShapeDtypeStruct(r.shape,...  3.39 us

profile of v5, /device:TPU:1, one launch (start us, length us, event | category | flops | bytes accessed | tf_op | source)
XLA Modules:
  0.0 119.6 jit_solution(3919305348550983187)
XLA Ops:
  0.6 115.6 %shard_map.211 = (f32[2,8,64,256]{3,2,1,0:T(8,128)}, f32[8,256]{1,0:T(8,128)}, f32[8,256]{1,0:T(8,128)}) custom-call(f32[2,8,64,256]{3,2,1,0:T(8,128)} %refs_0_.1, f32[8,64,256]{2,1,0:T(8,128)} %refs_1_.1, f32[2,8,64,256]{3,2,1,0:T(8,128)} %refs_2_.1, f32[2,16,128,512]{3,2,1,0:T(8,128)} %refs_3_.1, f32[8,256]{1,0:T(8,128)} %refs_4_.1, s32[2,16]{1,0:T(2,128)} %refs_5_.1, ...), custom_call_target="tpu_custom_call" | custom-call | tf_op jit(solution)/shard_map/pallas_call | solution.py:687
  116.3 3.4 %shard_map.212 = (f32[2,8,64,256]{3,2,1,0:T(8,128)}, f32[8,256]{1,0:T(8,128)}, f32[8,256]{1,0:T(8,128)}) custom-call(f32[2,8,64,256]{3,2,1,0:T(8,128)} %get-tuple-element.6.adj, f32[8,256]{1,0:T(8,128)} %get-tuple-element.7.proj, f32[8,256]{1,0:T(8,128)} %get-tuple-element.8.grad), custom_call_target="tpu_custom_call" | custom-call | tf_op jit(solution)/shard_map/pallas_call | solution.py:703
